TPU v7x, 512 devices: a whole 4x4x16 slice. The times are simulated.
512 devices in a mesh: ctx: 512 (over x, y, z, core).
Axes of the slice: x: 4, y: 4, z: 16, core: 2. Of those that a mesh axis runs over, the one named last changes fastest.
Arguments:
- query: bfloat16 [131072, 1280], P('ctx'), may hold values from -16 to 16
- key: bfloat16 [131072, 1280], P('ctx'), may hold values from -16 to 16
- value: bfloat16 [131072, 1280], P('ctx'), may hold values from -6 to 6
- grad_out: bfloat16 [131072, 1280], P('ctx'), may hold values from -16 to 16
- offsets: int32 [2, 10], replicated, may hold values from 0 to 255, as said below
Outputs:
- grad_query: bfloat16 [131072, 1280], P('ctx')
- grad_key: bfloat16 [131072, 1280], P('ctx')
- grad_value: bfloat16 [131072, 1280], P('ctx')
Inputs may be any that keep to these rules, and one draw needn't show every extreme that they name: Row 0 holds 0 or 1 for each head, half of the heads taking each; row 1 holds distinct offsets below 256, one of them 256 - 1.
All inputs are finite; a program needn't handle non-finite values.
Results may differ from a plain program's by a relative error of at most 0.007.
Values may be sent and summed in bfloat16 or wider, within the bound.
A program may use at most 64 MiB of HBM per device.

v0:
```python
import jax
import jax.numpy as jnp
from jax import lax
from jax.sharding import PartitionSpec as P


def swapped(block, axis, bit):
    count = lax.axis_size(axis)
    route = []
    for low in range(count):
        high = low | 1 << bit
        if high != low and high < count:
            route += [(low, high), (high, low)]
    return lax.ppermute(block, axis, route)


def selector_table(dilation, offset_row, dtype):
    return (
        lax.broadcasted_iota(jnp.int32, (dilation, offset_row.shape[0]), 0) == offset_row[None, :]
    ).astype(dtype)


def pick_rows(source, dilation, offset_row):
    length, head_count, head_size = source.shape
    selector = selector_table(dilation, offset_row, source.dtype)
    grouped = source.reshape(length // dilation, dilation, head_count, head_size)
    return jnp.sum(grouped * selector[None, :, :, None], axis=1)


def place_rows(source, dilation, offset_row):
    length, head_count, head_size = source.shape
    selector = selector_table(dilation, offset_row, source.dtype)
    return (source[:, None] * selector[None, :, :, None]).reshape(
        length * dilation, head_count, head_size
    )


def pick_stats(source, dilation, offset_row):
    head_count, length = source.shape
    selector = selector_table(dilation, offset_row, source.dtype)
    grouped = source.reshape(head_count, length // dilation, dilation)
    return jnp.sum(grouped * selector.T[:, None, :], axis=2)


def place_stats(source, dilation, offset_row):
    head_count, length = source.shape
    selector = selector_table(dilation, offset_row, source.dtype)
    return (source[:, :, None] * selector.T[:, None, :]).reshape(head_count, length * dilation)


def forward_level(queries, keys_in, values_in):
    factor = queries.shape[-1] ** (-0.5)
    scores = (
        jnp.einsum("mhc,nhc->hmn", queries, keys_in, preferred_element_type=jnp.float32) * factor
    )
    row_peak = jnp.max(scores, axis=-1)
    powered = jnp.exp(scores - row_peak[:, :, None])
    row_total = jnp.sum(powered, axis=-1)
    blended = jnp.einsum(
        "hmn,nhc->mhc", powered.astype(jnp.bfloat16), values_in, preferred_element_type=jnp.float32
    )
    return (row_peak, row_total, blended)


def backward_level(queries, keys_in, values_in, out_grads, log_total, row_delta):
    factor = queries.shape[-1] ** (-0.5)
    scores = (
        jnp.einsum("mhc,nhc->hmn", queries, keys_in, preferred_element_type=jnp.float32) * factor
    )
    chances = jnp.exp(scores - log_total[:, :, None])
    value_grad = jnp.einsum(
        "hmn,mhc->nhc", chances.astype(jnp.bfloat16), out_grads, preferred_element_type=jnp.float32
    )
    product_grad = jnp.einsum(
        "mhc,nhc->hmn", out_grads, values_in, preferred_element_type=jnp.float32
    )
    score_grad = (factor * chances * (product_grad - row_delta[:, :, None])).astype(jnp.bfloat16)
    query_grad = jnp.einsum("hmn,nhc->mhc", score_grad, keys_in, preferred_element_type=jnp.float32)
    key_grad = jnp.einsum("hmn,mhc->nhc", score_grad, queries, preferred_element_type=jnp.float32)
    return (query_grad, key_grad, value_grad)


def on_device(query, key, value, grad_out, offsets):
    length = query.shape[0]
    head_count = offsets.shape[1]
    head_size = query.shape[1] // head_count
    queries, keys_own, values_own, out_grads = [
        operand.reshape(length, head_count, head_size) for operand in (query, key, value, grad_out)
    ]
    span = min(lax.axis_size("ctx"), 128)
    doublings = span.bit_length() - 1
    pair_offsets = offsets[0]
    wide_offsets = offsets[1]
    half_rows = length // 2
    pair_parts = [
        pick_rows(operand, 2, pair_offsets)
        for operand in (keys_own, values_own, queries, out_grads)
    ]
    wide_parts = [
        pick_rows(operand, length, wide_offsets)
        for operand in (keys_own, values_own, queries, out_grads)
    ]
    pair_load = jnp.stack(pair_parts[:2], 1)
    wide_load = jnp.stack(wide_parts[:2], 1)
    pair_far = swapped(pair_load, "ctx", 0)
    wide_rows = wide_load
    for position in range(doublings):
        wide_rows = jnp.concatenate([wide_rows, swapped(wide_rows, "ctx", position)], 0)
    pair_keys = jnp.concatenate([pair_parts[0], pair_far[:, 0]], 0)
    pair_values = jnp.concatenate([pair_parts[1], pair_far[:, 1]], 0)
    wide_keys = wide_rows[:, 0]
    wide_values = wide_rows[:, 1]
    local_peak, local_total, local_blend = forward_level(queries, keys_own, values_own)
    pair_peak, pair_total, pair_blend = forward_level(pair_parts[2], pair_keys, pair_values)
    wide_peak, wide_total, wide_blend = forward_level(wide_parts[2], wide_keys, wide_values)
    pair_mask = place_stats(jnp.ones_like(pair_peak), 2, pair_offsets)
    wide_mask = place_stats(jnp.ones_like(wide_peak), length, wide_offsets)
    pair_peak_full = place_stats(pair_peak, 2, pair_offsets)
    wide_peak_full = place_stats(wide_peak, length, wide_offsets)
    row_peak = jnp.maximum(local_peak, jnp.where(pair_mask > 0, pair_peak_full, local_peak))
    row_peak = jnp.maximum(row_peak, jnp.where(wide_mask > 0, wide_peak_full, local_peak))
    local_weight = jnp.exp(local_peak - row_peak)
    pair_weight = pair_mask * jnp.exp(jnp.where(pair_mask > 0, pair_peak_full, row_peak) - row_peak)
    wide_weight = wide_mask * jnp.exp(jnp.where(wide_mask > 0, wide_peak_full, row_peak) - row_peak)
    row_total = (
        local_total * local_weight
        + place_stats(pair_total, 2, pair_offsets) * pair_weight
        + place_stats(wide_total, length, wide_offsets) * wide_weight
    )
    blended = (
        local_blend * local_weight.T[:, :, None]
        + place_rows(pair_blend, 2, pair_offsets) * pair_weight.T[:, :, None]
        + place_rows(wide_blend, length, wide_offsets) * wide_weight.T[:, :, None]
    )
    attended = blended / row_total.T[:, :, None]
    log_total = row_peak + jnp.log(row_total)
    row_delta = jnp.sum(out_grads.astype(jnp.float32) * attended, axis=-1).T
    local_query, local_key, local_value = backward_level(
        queries, keys_own, values_own, out_grads, log_total, row_delta
    )
    pair_log = pick_stats(log_total, 2, pair_offsets)
    pair_delta = pick_stats(row_delta, 2, pair_offsets)
    wide_log = pick_stats(log_total, length, wide_offsets)
    wide_delta = pick_stats(row_delta, length, wide_offsets)
    pair_query_grad, pair_key_part, pair_value_part = backward_level(
        pair_parts[2], pair_keys, pair_values, pair_parts[3], pair_log, pair_delta
    )
    pair_partial = jnp.stack([pair_key_part, pair_value_part], 1)
    pair_mine = pair_partial[:half_rows] + swapped(
        pair_partial[half_rows:].astype(jnp.bfloat16), "ctx", 0
    ).astype(jnp.float32)
    pair_key_grad = pair_mine[:, 0]
    pair_value_grad = pair_mine[:, 1]
    wide_query_grad, wide_key_part, wide_value_part = backward_level(
        wide_parts[2], wide_keys, wide_values, wide_parts[3], wide_log, wide_delta
    )
    wide_buffer = jnp.stack([wide_key_part, wide_value_part], 1)
    for position in reversed(range(doublings)):
        midpoint = wide_buffer.shape[0] // 2
        wide_buffer = wide_buffer[:midpoint] + swapped(
            wide_buffer[midpoint:].astype(jnp.bfloat16), "ctx", position
        ).astype(jnp.float32)
    wide_key_grad = wide_buffer[:, 0]
    wide_value_grad = wide_buffer[:, 1]
    query_sum = (
        local_query
        + place_rows(pair_query_grad, 2, pair_offsets)
        + place_rows(wide_query_grad, length, wide_offsets)
    )
    key_sum = (
        local_key
        + place_rows(pair_key_grad, 2, pair_offsets)
        + place_rows(wide_key_grad, length, wide_offsets)
    )
    value_sum = (
        local_value
        + place_rows(pair_value_grad, 2, pair_offsets)
        + place_rows(wide_value_grad, length, wide_offsets)
    )
    width_all = head_count * head_size
    return (
        query_sum.astype(jnp.bfloat16).reshape(length, width_all),
        key_sum.astype(jnp.bfloat16).reshape(length, width_all),
        value_sum.astype(jnp.bfloat16).reshape(length, width_all),
    )


def solution(mesh):
    placed = (P("ctx", None), P("ctx", None), P("ctx", None), P("ctx", None), P())
    return jax.shard_map(
        on_device,
        mesh=mesh,
        in_specs=placed,
        out_specs=(P("ctx", None), P("ctx", None), P("ctx", None)),
        check_vma=False,
    )
```

profile of v0, /device:TPU:1, one launch (start us, length us, event | category | flops | bytes accessed | tf_op | source)
XLA Modules:
  0.0 252.6 jit_solution(8786877944817460314)
XLA Ops:
  1.4 1.5 reshape_reshape.16
  5.7 2.2 reshape_reshape.19
  8.0 4.9 %multiply_reduce_fusion.5 = (bf16[128,10,128]{2,1,0:T(8,128)(2,1)}, bf16[128,10,128]{2,1,0:T(8,128)(2,1)S(1)}, bf16[128,10,128]{2,1,0:T(8,128)(2,1)S(1)}, bf16[128,10,128]{2,1,0:T(8,128)(2,1)}) fusion(bf16[128,2,10,128]{3,2,1,0:T(8,128)(2,1)} %reshape_reshape.19, bf16[2,10]{1,0:T(2,128)(2,1)S(1)} %get-tuple-element.72, ...), kind=kLoop, calls=%fused_computation.65 | loop fusion | flops 1966080 | bytes 3932200 | tf_op jit(solution)/shard_map/reduce_sum | solution.py:27
  14.1 8.9 %collective-permute-start = (bf16[128,2,10,128]{3,0,2,1:T(8,128)(2,1)}, bf16[128,2,10,128]{3,0,2,1:T(8,128)(2,1)}, u32[]{:S(2)}, u32[]{:S(2)}) collective-permute-start(bf16[128,2,10,128]{3,0,2,1:T(8,128)(2,1)} %pad_maximum_fusion.2), channel_id=1, source_target_pairs={{0,1},{1,0},{2,3},{3,2},{4,5},{5,4},{6,7},{7,6},{8,9},{9,8},{10,11... | collective-permute-start | bytes 1966088 | tf_op jit(solution)/shard_map/ppermute | solution.py:14
  23.7 1.6 copy.90
  27.4 1.9 collective-permute-start.1
  29.3 1.9 multiply_reduce_fusion
  31.3 2.1 collective-permute-start.2
  34.0 1.9 collective-permute-done.2
  35.9 1.9 collective-permute-start.3
  38.5 3.1 %collective-permute-done.3 = bf16[4,2,10,128]{3,2,1,0:T(8,128)(2,1)S(1)} collective-permute-done((bf16[4,2,10,128]{3,2,1,0:T(8,128)(2,1)S(1)}, bf16[4,2,10,128]{3,2,1,0:T(8,128)(2,1)S(1)}, u32[]{:S(2)}, u32[]{:S(2)}) %collective-permute-start.3) | collective-permute-done | bytes 20512 | tf_op jit(solution)/shard_map/ppermute | solution.py:14
  41.6 4.2 %collective-permute-start.4 = (bf16[8,2,10,128]{3,2,1,0:T(8,128)(2,1)S(1)}, bf16[8,2,10,128]{3,2,1,0:T(8,128)(2,1)S(1)}, u32[]{:S(2)}, u32[]{:S(2)}) collective-permute-start(bf16[8,2,10,128]{3,2,1,0:T(8,128)(2,1)S(1)} %pad_maximum_fusion.9), channel_id=1, source_target_pairs={{0,8},{8,0},{1,9},{9,1},{2,10},{10,2},{3,11},{11,3},{4,12},{12,4},... | collective-permute-start | bytes 122888 | tf_op jit(solution)/shard_map/ppermute | solution.py:14
  46.4 5.8 %collective-permute-done.4 = bf16[8,2,10,128]{3,2,1,0:T(8,128)(2,1)S(1)} collective-permute-done((bf16[8,2,10,128]{3,2,1,0:T(8,128)(2,1)S(1)}, bf16[8,2,10,128]{3,2,1,0:T(8,128)(2,1)S(1)}, u32[]{:S(2)}, u32[]{:S(2)}) %collective-permute-start.4) | collective-permute-done | bytes 40992 | tf_op jit(solution)/shard_map/ppermute | solution.py:14
  53.0 10.4 %collective-permute-start.5 = (bf16[16,2,10,128]{3,2,1,0:T(8,128)(2,1)}, bf16[16,2,10,128]{3,2,1,0:T(8,128)(2,1)}, u32[]{:S(2)}, u32[]{:S(2)}) collective-permute-start(bf16[16,2,10,128]{3,2,1,0:T(8,128)(2,1)} %get-tuple-element.44), channel_id=1, source_target_pairs={{0,16},{16,0},{1,17},{17,1},{2,18},{18,2},{3,19},{19,3},{4,20},{20... | collective-permute-start | bytes 245768 | tf_op jit(solution)/shard_map/ppermute | solution.py:14
  67.0 2.1 copy.114
  69.0 2.1 copy.113
  71.9 1.7 constant_dynamic-update-slice_fusion.12
  73.6 3.2 %collective-permute-start.6 = (bf16[32,2,10,128]{3,2,1,0:T(8,128)(2,1)}, bf16[32,2,10,128]{3,2,1,0:T(8,128)(2,1)}, u32[]{:S(2)}, u32[]{:S(2)}) collective-permute-start(bf16[32,2,10,128]{3,2,1,0:T(8,128)(2,1)} %get-tuple-element.36), channel_id=1, source_target_pairs={{0,32},{32,0},{1,33},{33,1},{2,34},{34,2},{3,35},{35,3},{4,36},{36... | collective-permute-start | bytes 491528 | tf_op jit(solution)/shard_map/ppermute | solution.py:14
  78.0 3.0 %collective-permute-done.6 = bf16[32,2,10,128]{3,2,1,0:T(8,128)(2,1)} collective-permute-done((bf16[32,2,10,128]{3,2,1,0:T(8,128)(2,1)}, bf16[32,2,10,128]{3,2,1,0:T(8,128)(2,1)}, u32[]{:S(2)}, u32[]{:S(2)}) %collective-permute-start.6) | collective-permute-done | bytes 163872 | tf_op jit(solution)/shard_map/ppermute | solution.py:14
  81.0 1.8 constant_dynamic-update-slice_fusion.11
  82.8 5.0 %collective-permute-start.7 = (bf16[64,2,10,128]{3,2,1,0:T(8,128)(2,1)}, bf16[64,2,10,128]{3,2,1,0:T(8,128)(2,1)S(1)}, u32[]{:S(2)}, u32[]{:S(2)}) collective-permute-start(bf16[64,2,10,128]{3,2,1,0:T(8,128)(2,1)} %get-tuple-element.32), channel_id=1, source_target_pairs={{0,64},{64,0},{1,65},{65,1},{2,66},{66,2},{3,67},{67,3},{4,68},{68... | collective-permute-start | bytes 983048 | tf_op jit(solution)/shard_map/ppermute | solution.py:14
  87.9 6.6 %collective-permute-done.7 = bf16[64,2,10,128]{3,2,1,0:T(8,128)(2,1)S(1)} collective-permute-done((bf16[64,2,10,128]{3,2,1,0:T(8,128)(2,1)}, bf16[64,2,10,128]{3,2,1,0:T(8,128)(2,1)S(1)}, u32[]{:S(2)}, u32[]{:S(2)}) %collective-permute-start.7) | collective-permute-done | bytes 327712 | tf_op jit(solution)/shard_map/ppermute | solution.py:14
  95.3 2.5 %multiply_reduce_fusion.2 = (f32[10,128]{0,1:T(8,128)}, f32[10,128]{0,1:T(8,128)S(1)}) fusion(f32[10,128]{1,0:T(8,128)S(1)} %get-tuple-element.79, bf16[128,2,10,128]{3,2,1,0:T(8,128)(2,1)} %constant_dynamic-update-slice_fusion.18, f32[10,128]{1,0:T(8,128)S(1)} %get-tuple-element.80), kind=kLoop, calls=%fused_computation.60 | loop fusion | flops 980480 | bytes 675840 | tf_op jit(solution)/shard_map/mhc,nhc->hmn/dot_general | solution.py:74
  99.4 1.9 slice_bitcast_fusion.2
  101.3 1.5 fusion.81
  103.4 2.4 fusion.32
  107.2 1.6 copy.81
  109.5 1.6 copy.87
  111.1 2.9 %convolution_bitcast_fusion.7 = f32[128,10,128]{0,2,1:T(8,128)} fusion(f32[10,128,256]{2,1,0:T(8,128)} %get-tuple-element.76, f32[10,128]{1,0:T(8,128)} %copy-done.33, bf16[128,10,128]{2,0,1:T(8,128)(2,1)} %get-tuple-element.30, bf16[128,10,128]{2,0,1:T(8,128)(2,1)} %copy.77), kind=kOutput, calls=%fused_computation.50 | convolution fusion | flops 85852160 | bytes 2626560 | tf_op jit(solution)/shard_map/hmn,nhc->mhc/dot_general | solution.py:59
  114.0 2.2 copy.97
  116.2 2.6 %mul.473 = f32[128,2,10,128]{3,1,0,2:T(2,128)} broadcast(f32[128,10,128]{2,0,1:T(8,128)} %copy.97), dimensions={0,2,3} | broadcast | bytes 1966080 | tf_op jit(solution)/shard_map/mul | solution.py:33
  118.8 2.8 %copy.99 = f32[256,10,128]{0,2,1:T(8,128)} copy(f32[256,10,128]{2,0,1:T(8,128)} %bitcast.165) | data formatting | bytes 2621440 | tf_op jit(solution)/shard_map/mul | solution.py:33
  121.6 1.5 log_add_fusion.1
  123.9 2.5 fusion.28
  127.7 1.5 copy.106
  129.2 2.7 %fusion.55 = (f32[10]{0:T(128)}, f32[10,128]{0,1:T(8,128)}, f32[10,128]{0,1:T(8,128)}) fusion(s32[10]{0:T(128)} %copy-done.38, s32[128,2]{1,0:T(8,128)S(1)} %multiply_add_fusion, f32[10,2]{0,1:T(2,128)} %copy-done.41, f32[10,128,2]{0,2,1:T(2,128)} %bitcast.176, f32[10]{0:T(128)} %get-tuple-element.40, f32[10,128]{0,1:T(8,128)S(1)} %copy.86, ...), kind=kLoop, calls=%fused_computation.104 | loop fusion | flops 74230 | bytes 52484 | tf_op jit(solution)/shard_map/reduce_sum | solution.py:42
  135.5 5.0 %collective-permute-start.9 = (bf16[64,2,10,128]{3,2,1,0:T(8,128)(2,1)S(1)}, bf16[64,2,10,128]{3,2,1,0:T(8,128)(2,1)S(1)}, u32[]{:S(2)}, u32[]{:S(2)}) collective-permute-start(bf16[64,2,10,128]{3,2,1,0:T(8,128)(2,1)S(1)} %fusion.36), channel_id=1, source_target_pairs={{0,64},{64,0},{1,65},{65,1},{2,66},{66,2},{3,67},{67,3},{4,68},{68... | collective-permute-start | bytes 983048 | tf_op jit(solution)/shard_map/ppermute | solution.py:14
  141.1 2.0 multiply_convert_fusion
  143.1 3.9 %collective-permute-done.9 = bf16[64,2,10,128]{3,2,1,0:T(8,128)(2,1)S(1)} collective-permute-done((bf16[64,2,10,128]{3,2,1,0:T(8,128)(2,1)S(1)}, bf16[64,2,10,128]{3,2,1,0:T(8,128)(2,1)S(1)}, u32[]{:S(2)}, u32[]{:S(2)}) %collective-permute-start.9) | collective-permute-done | bytes 327712 | tf_op jit(solution)/shard_map/ppermute | solution.py:14
  147.2 3.2 %collective-permute-start.10 = (bf16[32,2,10,128]{3,2,1,0:T(8,128)(2,1)S(1)}, bf16[32,2,10,128]{3,2,1,0:T(8,128)(2,1)S(1)}, u32[]{:S(2)}, u32[]{:S(2)}) collective-permute-start(bf16[32,2,10,128]{3,2,1,0:T(8,128)(2,1)S(1)} %slice.176), channel_id=1, source_target_pairs={{0,32},{32,0},{1,33},{33,1},{2,34},{34,2},{3,35},{35,3},{4,36},{36... | collective-permute-start | bytes 491528 | tf_op jit(solution)/shard_map/ppermute | solution.py:14
  151.7 5.8 %collective-permute-done.10 = bf16[32,2,10,128]{3,2,1,0:T(8,128)(2,1)S(1)} collective-permute-done((bf16[32,2,10,128]{3,2,1,0:T(8,128)(2,1)S(1)}, bf16[32,2,10,128]{3,2,1,0:T(8,128)(2,1)S(1)}, u32[]{:S(2)}, u32[]{:S(2)}) %collective-permute-start.10) | collective-permute-done | bytes 163872 | tf_op jit(solution)/shard_map/ppermute | solution.py:14
  157.6 9.2 %collective-permute-start.11 = (bf16[16,2,10,128]{3,2,1,0:T(8,128)(2,1)S(1)}, bf16[16,2,10,128]{3,2,1,0:T(8,128)(2,1)S(1)}, u32[]{:S(2)}, u32[]{:S(2)}) collective-permute-start(bf16[16,2,10,128]{3,2,1,0:T(8,128)(2,1)S(1)} %slice.177), channel_id=1, source_target_pairs={{0,16},{16,0},{1,17},{17,1},{2,18},{18,2},{3,19},{19,3},{4,20},{20... | collective-permute-start | bytes 245768 | tf_op jit(solution)/shard_map/ppermute | solution.py:14
  167.2 4.9 %collective-permute-done.11 = bf16[16,2,10,128]{3,2,1,0:T(8,128)(2,1)S(1)} collective-permute-done((bf16[16,2,10,128]{3,2,1,0:T(8,128)(2,1)S(1)}, bf16[16,2,10,128]{3,2,1,0:T(8,128)(2,1)S(1)}, u32[]{:S(2)}, u32[]{:S(2)}) %collective-permute-start.11) | collective-permute-done | bytes 81952 | tf_op jit(solution)/shard_map/ppermute | solution.py:14
  172.2 2.1 collective-permute-start.12
  174.6 6.9 %collective-permute-done.12 = bf16[8,2,10,128]{3,2,1,0:T(8,128)(2,1)S(1)} collective-permute-done((bf16[8,2,10,128]{3,2,1,0:T(8,128)(2,1)S(1)}, bf16[8,2,10,128]{3,2,1,0:T(8,128)(2,1)S(1)}, u32[]{:S(2)}, u32[]{:S(2)}) %collective-permute-start.12) | collective-permute-done | bytes 40992 | tf_op jit(solution)/shard_map/ppermute | solution.py:14
  181.6 11.3 %collective-permute-start.13 = (bf16[4,2,10,128]{3,2,1,0:T(8,128)(2,1)S(1)}, bf16[4,2,10,128]{3,2,1,0:T(8,128)(2,1)S(1)}, u32[]{:S(2)}, u32[]{:S(2)}) collective-permute-start(bf16[4,2,10,128]{3,2,1,0:T(8,128)(2,1)S(1)} %slice.179), channel_id=1, source_target_pairs={{0,4},{4,0},{1,5},{5,1},{2,6},{6,2},{3,7},{7,3},{8,12},{12,8},{9,1... | collective-permute-start | bytes 61448 | tf_op jit(solution)/shard_map/ppermute | solution.py:14
  194.2 6.9 %collective-permute-start.14 = (bf16[2,2,10,128]{3,2,1,0:T(8,128)(2,1)S(1)}, bf16[2,2,10,128]{3,2,1,0:T(8,128)(2,1)S(1)}, u32[]{:S(2)}, u32[]{:S(2)}) collective-permute-start(bf16[2,2,10,128]{3,2,1,0:T(8,128)(2,1)S(1)} %slice.180), channel_id=1, source_target_pairs={{0,2},{2,0},{1,3},{3,1},{4,6},{6,4},{5,7},{7,5},{8,10},{10,8},{9,1... | collective-permute-start | bytes 30728 | tf_op jit(solution)/shard_map/ppermute | solution.py:14
  202.1 2.2 copy.109
  204.2 2.6 %mul.505 = f32[128,2,10,128]{3,1,0,2:T(2,128)} broadcast(f32[128,10,128]{2,0,1:T(8,128)} %copy.109), dimensions={0,2,3} | broadcast | bytes 1966080 | tf_op jit(solution)/shard_map/mul | solution.py:33
  206.9 2.8 %copy.110 = f32[256,10,128]{0,2,1:T(8,128)} copy(f32[256,10,128]{2,0,1:T(8,128)} %bitcast.166) | data formatting | bytes 2621440 | tf_op jit(solution)/shard_map/mul | solution.py:33
  209.7 9.1 %collective-permute-start.8 = (bf16[128,2,10,128]{0,3,2,1:T(8,128)(2,1)}, bf16[128,2,10,128]{0,3,2,1:T(8,128)(2,1)}, u32[]{:S(2)}, u32[]{:S(2)}) collective-permute-start(bf16[128,2,10,128]{0,3,2,1:T(8,128)(2,1)} %fusion.23), channel_id=1, source_target_pairs={{0,1},{1,0},{2,3},{3,2},{4,5},{5,4},{6,7},{7,6},{8,9},{9,8},{10,11... | collective-permute-start | bytes 1966088 | tf_op jit(solution)/shard_map/ppermute | solution.py:14
  218.8 2.1 collective-permute-start.15
  221.0 3.2 %fusion.17 = bf16[256,10,128]{0,2,1:T(8,128)(2,1)} fusion(bf16[256,10,128]{0,2,1:T(8,128)(2,1)} %bitcast.162, bf16[10,256,256]{1,2,0:T(8,128)(2,1)} %multiply_convert_fusion, f32[256,10,128]{0,2,1:T(8,128)} %copy.110, f32[10,128]{1,0:T(8,128)S(1)} %multiply_reduce_fusion.1, f32[256,10]{0,1:T(8,128)S(1)} %copy-done.28, f32[256,10]{0,1:T(8,128)S(1)} %copy-done.27), kind=kOutput, calls=%fused_computation.37 | convolution fusion | flops 169410560 | bytes 3957760 | tf_op jit(solution)/shard_map/hmn,nhc->mhc/dot_general | solution.py:78
  224.1 2.2 copy.120
  226.3 1.6 fusion.22
  229.2 2.2 copy.118
  231.3 2.6 %mul.523 = f32[128,2,10,128]{3,1,0,2:T(2,128)} broadcast(f32[128,10,128]{2,0,1:T(8,128)} %copy.118), dimensions={0,2,3} | broadcast | bytes 1966080 | tf_op jit(solution)/shard_map/mul | solution.py:33
  233.9 2.8 %copy.119 = f32[256,10,128]{0,2,1:T(8,128)} copy(f32[256,10,128]{2,0,1:T(8,128)} %bitcast.167) | data formatting | bytes 2621440 | tf_op jit(solution)/shard_map/mul | solution.py:33
  236.7 2.2 copy.115
  238.9 2.6 %mul.516 = f32[128,2,10,128]{3,1,0,2:T(2,128)} broadcast(f32[128,10,128]{2,0,1:T(8,128)} %copy.115), dimensions={0,2,3} | broadcast | bytes 1966080 | tf_op jit(solution)/shard_map/mul | solution.py:33
  241.5 2.8 %copy.116 = f32[256,10,128]{0,2,1:T(8,128)} copy(f32[256,10,128]{2,0,1:T(8,128)} %bitcast.168) | data formatting | bytes 2621440 | tf_op jit(solution)/shard_map/mul | solution.py:33
  244.2 2.9 %fusion.16 = bf16[256,10,128]{0,2,1:T(8,128)(2,1)} fusion(bf16[256,10,128]{0,2,1:T(8,128)(2,1)S(1)} %bitcast.158, f32[10,256,256]{1,2,0:T(8,128)S(1)} %get-tuple-element.78, f32[256,10,128]{0,2,1:T(8,128)} %copy.119, f32[10,256]{1,0:T(8,128)S(1)} %copy-done.32, f32[10,128]{1,0:T(8,128)S(1)} %get-tuple-element.49, f32[256,10]{0,1:T(8,128)S(1)} %copy-done.28, ...), kind=kOutput, calls=%fused_computation.36 | convolution fusion | flops 171376640 | bytes 5278720 | tf_op jit(solution)/shard_map/hmn,mhc->nhc/dot_general | solution.py:71
  247.1 2.3 copy.122
  249.4 2.1 fusion.15
  (163 shorter events, 34.2 us)
Async XLA Ops:
  0.6 2.3 copy-start.21
  1.4 23.9 %copy-start.38 = (s32[10]{0:T(128)}, s32[10]{0:T(128)S(1)}, u32[]{:S(2)}) copy-start(s32[10]{0:T(128)S(1)} %get-tuple-element.67) | copy-start | bytes 124
  1.4 2.9 %copy-start.22 = (bf16[256,1280]{1,0:T(8,128)(2,1)S(1)}, bf16[256,1280]{1,0:T(8,128)(2,1)}, u32[]{:S(2)}) copy-start(bf16[256,1280]{1,0:T(8,128)(2,1)} %param.7) | copy-start | bytes 1966084
  12.9 1.1 copy-start.8
  12.9 1.2 copy-start.10
  12.9 10.1 %copy-start.20 = (bf16[256,1280]{1,0:T(8,128)(2,1)S(1)}, bf16[256,1280]{1,0:T(8,128)(2,1)}, u32[]{:S(2)}) copy-start(bf16[256,1280]{1,0:T(8,128)(2,1)} %param.5) | copy-start | bytes 1966084
  14.1 9.4 %copy-start.23 = (bf16[256,1280]{1,0:T(8,128)(2,1)S(1)}, bf16[256,1280]{1,0:T(8,128)(2,1)}, u32[]{:S(2)}) copy-start(bf16[256,1280]{1,0:T(8,128)(2,1)} %param.7) | copy-start | bytes 1966084
  14.1 85.3 %collective-permute-start = (bf16[128,2,10,128]{3,0,2,1:T(8,128)(2,1)}, bf16[128,2,10,128]{3,0,2,1:T(8,128)(2,1)}, u32[]{:S(2)}, u32[]{:S(2)}) collective-permute-start(bf16[128,2,10,128]{3,0,2,1:T(8,128)(2,1)} %pad_maximum_fusion.2), channel_id=1, source_target_pairs={{0,1},{1,0},{2,3},{3,2},{4,5},{5,4},{6,7},{7,6},{8,9},{9,8},{10,11... | collective-permute-start | bytes 1966088 | tf_op jit(solution)/shard_map/ppermute | solution.py:14
  23.2 2.8 %copy-start.4 = (bf16[256,1280]{0,1:T(8,128)(2,1)}, bf16[256,1280]{0,1:T(8,128)(2,1)S(1)}, u32[]{:S(2)}) copy-start(bf16[256,1280]{0,1:T(8,128)(2,1)S(1)} %copy.71) | copy-start | bytes 1966084
  23.5 2.5 copy-start.5
  23.7 3.0 %copy-start.6 = (bf16[256,1280]{0,1:T(8,128)(2,1)}, bf16[256,1280]{0,1:T(8,128)(2,1)S(1)}, u32[]{:S(2)}) copy-start(bf16[256,1280]{0,1:T(8,128)(2,1)S(1)} %copy.85) | copy-start | bytes 1966084
  27.4 3.9 %collective-permute-start.1 = (bf16[1,2,10,128]{3,2,1,0:T(8,128)(2,1)S(1)}, bf16[1,2,10,128]{3,2,1,0:T(8,128)(2,1)S(1)}, u32[]{:S(2)}, u32[]{:S(2)}) collective-permute-start(bf16[1,2,10,128]{3,2,1,0:T(8,128)(2,1)S(1)} %get-tuple-element.66), channel_id=1, source_target_pairs={{0,1},{1,0},{2,3},{3,2},{4,5},{5,4},{6,7},{7,6},{8,9},{9,8},{10,11... | collective-permute-start | bytes 15368 | tf_op jit(solution)/shard_map/ppermute | solution.py:14
  29.3 34.6 %copy-start.11 = (bf16[128,10,128]{2,1,0:T(8,128)(2,1)S(1)}, bf16[128,10,128]{2,1,0:T(8,128)(2,1)}, u32[]{:S(2)}) copy-start(bf16[128,10,128]{2,1,0:T(8,128)(2,1)} %copy-done.10) | copy-start | bytes 983044
  31.2 33.5 %copy-start.9 = (bf16[128,10,128]{2,1,0:T(8,128)(2,1)S(1)}, bf16[128,10,128]{2,1,0:T(8,128)(2,1)}, u32[]{:S(2)}) copy-start(bf16[128,10,128]{2,1,0:T(8,128)(2,1)} %copy-done.8) | copy-start | bytes 983044
  31.3 4.6 %collective-permute-start.2 = (bf16[2,2,10,128]{3,2,1,0:T(8,128)(2,1)S(1)}, bf16[2,2,10,128]{3,2,1,0:T(8,128)(2,1)S(1)}, u32[]{:S(2)}, u32[]{:S(2)}) collective-permute-start(bf16[2,2,10,128]{3,2,1,0:T(8,128)(2,1)S(1)} %pad_maximum_fusion.11), channel_id=1, source_target_pairs={{0,2},{2,0},{1,3},{3,1},{4,6},{6,4},{5,7},{7,5},{8,10},{10,8},{9,1... | collective-permute-start | bytes 30728 | tf_op jit(solution)/shard_map/ppermute | solution.py:14
  35.9 5.6 %collective-permute-start.3 = (bf16[4,2,10,128]{3,2,1,0:T(8,128)(2,1)S(1)}, bf16[4,2,10,128]{3,2,1,0:T(8,128)(2,1)S(1)}, u32[]{:S(2)}, u32[]{:S(2)}) collective-permute-start(bf16[4,2,10,128]{3,2,1,0:T(8,128)(2,1)S(1)} %pad_maximum_fusion.10), channel_id=1, source_target_pairs={{0,4},{4,0},{1,5},{5,1},{2,6},{6,2},{3,7},{7,3},{8,12},{12,8},{9,1... | collective-permute-start | bytes 61448 | tf_op jit(solution)/shard_map/ppermute | solution.py:14
  41.6 10.7 %collective-permute-start.4 = (bf16[8,2,10,128]{3,2,1,0:T(8,128)(2,1)S(1)}, bf16[8,2,10,128]{3,2,1,0:T(8,128)(2,1)S(1)}, u32[]{:S(2)}, u32[]{:S(2)}) collective-permute-start(bf16[8,2,10,128]{3,2,1,0:T(8,128)(2,1)S(1)} %pad_maximum_fusion.9), channel_id=1, source_target_pairs={{0,8},{8,0},{1,9},{9,1},{2,10},{10,2},{3,11},{11,3},{4,12},{12,4},... | collective-permute-start | bytes 122888 | tf_op jit(solution)/shard_map/ppermute | solution.py:14
  53.0 12.6 %copy-start.42 = (bf16[32,2,10,128]{3,2,1,0:T(8,128)(2,1)}, bf16[32,2,10,128]{3,2,1,0:T(8,128)(2,1)S(1)}, u32[]{:S(2)}) copy-start(bf16[32,2,10,128]{3,2,1,0:T(8,128)(2,1)S(1)} %get-tuple-element.43) | copy-start | bytes 491524
  53.0 18.9 %collective-permute-start.5 = (bf16[16,2,10,128]{3,2,1,0:T(8,128)(2,1)}, bf16[16,2,10,128]{3,2,1,0:T(8,128)(2,1)}, u32[]{:S(2)}, u32[]{:S(2)}) collective-permute-start(bf16[16,2,10,128]{3,2,1,0:T(8,128)(2,1)} %get-tuple-element.44), channel_id=1, source_target_pairs={{0,16},{16,0},{1,17},{17,1},{2,18},{18,2},{3,19},{19,3},{4,20},{20... | collective-permute-start | bytes 245768 | tf_op jit(solution)/shard_map/ppermute | solution.py:14
  63.9 5.1 %copy-start.41 = (f32[10,2]{0,1:T(2,128)}, f32[10,2]{0,1:T(2,128)S(1)}, u32[]{:S(2)}) copy-start(f32[10,2]{0,1:T(2,128)S(1)} %get-tuple-element.70) | copy-start | bytes 244
  73.6 7.4 %collective-permute-start.6 = (bf16[32,2,10,128]{3,2,1,0:T(8,128)(2,1)}, bf16[32,2,10,128]{3,2,1,0:T(8,128)(2,1)}, u32[]{:S(2)}, u32[]{:S(2)}) collective-permute-start(bf16[32,2,10,128]{3,2,1,0:T(8,128)(2,1)} %get-tuple-element.36), channel_id=1, source_target_pairs={{0,32},{32,0},{1,33},{33,1},{2,34},{34,2},{3,35},{35,3},{4,36},{36... | collective-permute-start | bytes 491528 | tf_op jit(solution)/shard_map/ppermute | solution.py:14
  77.2 18.1 %copy-start.31 = (f32[10,256]{1,0:T(8,128)}, f32[10,256]{1,0:T(8,128)S(1)}, u32[]{:S(2)}) copy-start(f32[10,256]{1,0:T(8,128)S(1)} %fusion.1) | copy-start | bytes 30724
  82.8 11.6 %collective-permute-start.7 = (bf16[64,2,10,128]{3,2,1,0:T(8,128)(2,1)}, bf16[64,2,10,128]{3,2,1,0:T(8,128)(2,1)S(1)}, u32[]{:S(2)}, u32[]{:S(2)}) collective-permute-start(bf16[64,2,10,128]{3,2,1,0:T(8,128)(2,1)} %get-tuple-element.32), channel_id=1, source_target_pairs={{0,64},{64,0},{1,65},{65,1},{2,66},{66,2},{3,67},{67,3},{4,68},{68... | collective-permute-start | bytes 983048 | tf_op jit(solution)/shard_map/ppermute | solution.py:14
  87.9 10.0 %copy-start.34 = (f32[10,128]{1,0:T(8,128)}, f32[10,128]{1,0:T(8,128)S(1)}, u32[]{:S(2)}) copy-start(f32[10,128]{1,0:T(8,128)S(1)} %get-tuple-element.80) | copy-start | bytes 15364
  87.9 10.0 %copy-start.36 = (f32[10,128]{1,0:T(8,128)}, f32[10,128]{1,0:T(8,128)S(1)}, u32[]{:S(2)}) copy-start(f32[10,128]{1,0:T(8,128)S(1)} %get-tuple-element.79) | copy-start | bytes 15364
  95.3 3.2 %copy-start.12 = (bf16[128,2,10,128]{3,2,1,0:T(8,128)(2,1)S(1)}, bf16[128,2,10,128]{3,2,1,0:T(8,128)(2,1)}, u32[]{:S(2)}) copy-start(bf16[128,2,10,128]{3,2,1,0:T(8,128)(2,1)} %constant_dynamic-update-slice_fusion.18) | copy-start | bytes 1966084
  97.8 3.5 %copy-start.14 = (bf16[128,10,128]{0,2,1:T(8,128)(2,1)S(1)}, bf16[128,10,128]{0,2,1:T(8,128)(2,1)}, u32[]{:S(2)}) copy-start(bf16[128,10,128]{0,2,1:T(8,128)(2,1)} %copy.113) | copy-start | bytes 983044
  97.8 3.5 %copy-start.18 = (bf16[128,10,128]{2,0,1:T(8,128)(2,1)S(1)}, bf16[128,10,128]{2,0,1:T(8,128)(2,1)}, u32[]{:S(2)}) copy-start(bf16[128,10,128]{2,0,1:T(8,128)(2,1)} %copy.78) | copy-start | bytes 983044
  97.9 3.4 %copy-start.40 = (f32[10]{0:T(128)}, f32[10]{0:T(128)S(1)}, u32[]{:S(2)}) copy-start(f32[10]{0:T(128)S(1)} %multiply_reduce_fusion.11) | copy-start | bytes 124
  101.3 1.5 copy-start.16
  102.8 0.6 copy-start.33
  123.9 3.1 %copy-start.39 = (s32[10]{0:T(128)S(1)}, s32[10]{0:T(128)}, u32[]{:S(2)}) copy-start(s32[10]{0:T(128)} %copy-done.38) | copy-start | bytes 124
  126.4 0.6 copy-start.29
  127.0 7.7 %copy-start.37 = (f32[10,128]{1,0:T(8,128)S(1)}, f32[10,128]{1,0:T(8,128)}, u32[]{:S(2)}) copy-start(f32[10,128]{1,0:T(8,128)} %copy-done.36) | copy-start | bytes 15364
  127.0 8.0 %copy-start.35 = (f32[10,128]{1,0:T(8,128)S(1)}, f32[10,128]{1,0:T(8,128)}, u32[]{:S(2)}) copy-start(f32[10,128]{1,0:T(8,128)} %copy-done.34) | copy-start | bytes 15364
  135.3 5.1 %copy-start = (f32[10,128,256]{2,1,0:T(8,128)S(1)}, f32[10,128,256]{2,1,0:T(8,128)}, u32[]{:S(2)}) copy-start(f32[10,128,256]{2,1,0:T(8,128)} %get-tuple-element.76) | copy-start | bytes 3932164
  135.3 5.1 %copy-start.24 = (bf16[128,10,128]{2,0,1:T(8,128)(2,1)S(1)}, bf16[128,10,128]{2,0,1:T(8,128)(2,1)}, u32[]{:S(2)}) copy-start(bf16[128,10,128]{2,0,1:T(8,128)(2,1)} %get-tuple-element.30) | copy-start | bytes 983044
  135.3 5.1 %copy-start.25 = (bf16[128,10,128]{2,0,1:T(8,128)(2,1)S(1)}, bf16[128,10,128]{2,0,1:T(8,128)(2,1)}, u32[]{:S(2)}) copy-start(bf16[128,10,128]{2,0,1:T(8,128)(2,1)} %copy.77) | copy-start | bytes 983044
  135.4 5.1 %copy-start.26 = (bf16[128,10,128]{0,2,1:T(8,128)(2,1)S(1)}, bf16[128,10,128]{0,2,1:T(8,128)(2,1)}, u32[]{:S(2)}) copy-start(bf16[128,10,128]{0,2,1:T(8,128)(2,1)} %copy.114) | copy-start | bytes 983044
  135.4 5.6 %copy-start.7 = (bf16[256,1280]{0,1:T(8,128)(2,1)S(1)}, bf16[256,1280]{0,1:T(8,128)(2,1)}, u32[]{:S(2)}) copy-start(bf16[256,1280]{0,1:T(8,128)(2,1)} %copy-done.6) | copy-start | bytes 1966084
  135.5 5.6 %copy-start.30 = (f32[256,10]{0,1:T(8,128)S(1)}, f32[256,10]{0,1:T(8,128)}, u32[]{:S(2)}) copy-start(f32[256,10]{0,1:T(8,128)} %copy-done.29) | copy-start | bytes 30724
  135.5 5.6 %copy-start.32 = (f32[10,256]{1,0:T(8,128)S(1)}, f32[10,256]{1,0:T(8,128)}, u32[]{:S(2)}) copy-start(f32[10,256]{1,0:T(8,128)} %get-tuple-element.25) | copy-start | bytes 30724
  135.5 11.6 %collective-permute-start.9 = (bf16[64,2,10,128]{3,2,1,0:T(8,128)(2,1)S(1)}, bf16[64,2,10,128]{3,2,1,0:T(8,128)(2,1)S(1)}, u32[]{:S(2)}, u32[]{:S(2)}) collective-permute-start(bf16[64,2,10,128]{3,2,1,0:T(8,128)(2,1)S(1)} %fusion.36), channel_id=1, source_target_pairs={{0,64},{64,0},{1,65},{65,1},{2,66},{66,2},{3,67},{67,3},{4,68},{68... | collective-permute-start | bytes 983048 | tf_op jit(solution)/shard_map/ppermute | solution.py:14
  143.1 7.4 %copy-start.17 = (bf16[128,10,128]{2,0,1:T(8,128)(2,1)S(1)}, bf16[128,10,128]{2,0,1:T(8,128)(2,1)}, u32[]{:S(2)}) copy-start(bf16[128,10,128]{2,0,1:T(8,128)(2,1)} %copy-done.16) | copy-start | bytes 983044
  143.1 7.4 %copy-start.19 = (bf16[128,10,128]{2,0,1:T(8,128)(2,1)S(1)}, bf16[128,10,128]{2,0,1:T(8,128)(2,1)}, u32[]{:S(2)}) copy-start(bf16[128,10,128]{2,0,1:T(8,128)(2,1)} %copy.78) | copy-start | bytes 983044
  147.2 10.2 %collective-permute-start.10 = (bf16[32,2,10,128]{3,2,1,0:T(8,128)(2,1)S(1)}, bf16[32,2,10,128]{3,2,1,0:T(8,128)(2,1)S(1)}, u32[]{:S(2)}, u32[]{:S(2)}) collective-permute-start(bf16[32,2,10,128]{3,2,1,0:T(8,128)(2,1)S(1)} %slice.176), channel_id=1, source_target_pairs={{0,32},{32,0},{1,33},{33,1},{2,34},{34,2},{3,35},{35,3},{4,36},{36... | collective-permute-start | bytes 491528 | tf_op jit(solution)/shard_map/ppermute | solution.py:14
  157.6 16.7 %copy-start.15 = (bf16[128,10,128]{0,2,1:T(8,128)(2,1)S(1)}, bf16[128,10,128]{0,2,1:T(8,128)(2,1)}, u32[]{:S(2)}) copy-start(bf16[128,10,128]{0,2,1:T(8,128)(2,1)} %copy.113) | copy-start | bytes 983044
  157.6 14.6 %collective-permute-start.11 = (bf16[16,2,10,128]{3,2,1,0:T(8,128)(2,1)S(1)}, bf16[16,2,10,128]{3,2,1,0:T(8,128)(2,1)S(1)}, u32[]{:S(2)}, u32[]{:S(2)}) collective-permute-start(bf16[16,2,10,128]{3,2,1,0:T(8,128)(2,1)S(1)} %slice.177), channel_id=1, source_target_pairs={{0,16},{16,0},{1,17},{17,1},{2,18},{18,2},{3,19},{19,3},{4,20},{20... | collective-permute-start | bytes 245768 | tf_op jit(solution)/shard_map/ppermute | solution.py:14
  167.2 33.9 %copy-start.2 = (f32[256,1,10,128]{0,3,2,1:T(8,128)}, f32[256,1,10,128]{0,3,2,1:T(8,128)S(1)}, u32[]{:S(2)}) copy-start(f32[256,1,10,128]{0,3,2,1:T(8,128)S(1)} %convolution_bitcast_fusion.4) | copy-start | bytes 3932164
  172.2 20.7 %copy-start.13 = (bf16[128,2,10,128]{3,2,1,0:T(8,128)(2,1)S(1)}, bf16[128,2,10,128]{3,2,1,0:T(8,128)(2,1)}, u32[]{:S(2)}) copy-start(bf16[128,2,10,128]{3,2,1,0:T(8,128)(2,1)} %constant_dynamic-update-slice_fusion.18) | copy-start | bytes 1966084
  172.2 9.4 %collective-permute-start.12 = (bf16[8,2,10,128]{3,2,1,0:T(8,128)(2,1)S(1)}, bf16[8,2,10,128]{3,2,1,0:T(8,128)(2,1)S(1)}, u32[]{:S(2)}, u32[]{:S(2)}) collective-permute-start(bf16[8,2,10,128]{3,2,1,0:T(8,128)(2,1)S(1)} %slice.178), channel_id=1, source_target_pairs={{0,8},{8,0},{1,9},{9,1},{2,10},{10,2},{3,11},{11,3},{4,12},{12,4},... | collective-permute-start | bytes 122888 | tf_op jit(solution)/shard_map/ppermute | solution.py:14
  174.6 26.5 %copy-start.3 = (f32[256,1,10,128]{0,3,2,1:T(8,128)}, f32[256,1,10,128]{0,3,2,1:T(8,128)S(1)}, u32[]{:S(2)}) copy-start(f32[256,1,10,128]{0,3,2,1:T(8,128)S(1)} %convolution_bitcast_fusion.5) | copy-start | bytes 3932164
  181.6 12.6 %collective-permute-start.13 = (bf16[4,2,10,128]{3,2,1,0:T(8,128)(2,1)S(1)}, bf16[4,2,10,128]{3,2,1,0:T(8,128)(2,1)S(1)}, u32[]{:S(2)}, u32[]{:S(2)}) collective-permute-start(bf16[4,2,10,128]{3,2,1,0:T(8,128)(2,1)S(1)} %slice.179), channel_id=1, source_target_pairs={{0,4},{4,0},{1,5},{5,1},{2,6},{6,2},{3,7},{7,3},{8,12},{12,8},{9,1... | collective-permute-start | bytes 61448 | tf_op jit(solution)/shard_map/ppermute | solution.py:14
  194.2 24.6 %collective-permute-start.14 = (bf16[2,2,10,128]{3,2,1,0:T(8,128)(2,1)S(1)}, bf16[2,2,10,128]{3,2,1,0:T(8,128)(2,1)S(1)}, u32[]{:S(2)}, u32[]{:S(2)}) collective-permute-start(bf16[2,2,10,128]{3,2,1,0:T(8,128)(2,1)S(1)} %slice.180), channel_id=1, source_target_pairs={{0,2},{2,0},{1,3},{3,1},{4,6},{6,4},{5,7},{7,5},{8,10},{10,8},{9,1... | collective-permute-start | bytes 30728 | tf_op jit(solution)/shard_map/ppermute | solution.py:14
  206.9 14.1 %copy-start.27 = (f32[256,10]{0,1:T(8,128)S(1)}, f32[256,10]{0,1:T(8,128)}, u32[]{:S(2)}) copy-start(f32[256,10]{0,1:T(8,128)} %copy.98) | copy-start | bytes 30724
  206.9 14.1 %copy-start.28 = (f32[256,10]{0,1:T(8,128)S(1)}, f32[256,10]{0,1:T(8,128)}, u32[]{:S(2)}) copy-start(f32[256,10]{0,1:T(8,128)} %get-tuple-element.73) | copy-start | bytes 30724
  209.7 16.6 %collective-permute-start.8 = (bf16[128,2,10,128]{0,3,2,1:T(8,128)(2,1)}, bf16[128,2,10,128]{0,3,2,1:T(8,128)(2,1)}, u32[]{:S(2)}, u32[]{:S(2)}) collective-permute-start(bf16[128,2,10,128]{0,3,2,1:T(8,128)(2,1)} %fusion.23), channel_id=1, source_target_pairs={{0,1},{1,0},{2,3},{3,2},{4,5},{5,4},{6,7},{7,6},{8,9},{9,8},{10,11... | collective-permute-start | bytes 1966088 | tf_op jit(solution)/shard_map/ppermute | solution.py:14
  218.8 7.5 %collective-permute-start.15 = (bf16[1,2,10,128]{3,2,1,0:T(8,128)(2,1)S(1)}, bf16[1,2,10,128]{3,2,1,0:T(8,128)(2,1)S(1)}, u32[]{:S(2)}, u32[]{:S(2)}) collective-permute-start(bf16[1,2,10,128]{3,2,1,0:T(8,128)(2,1)S(1)} %slice.181), channel_id=1, source_target_pairs={{0,1},{1,0},{2,3},{3,2},{4,5},{5,4},{6,7},{7,6},{8,9},{9,8},{10,11... | collective-permute-start | bytes 15368 | tf_op jit(solution)/shard_map/ppermute | solution.py:14
  247.1 2.3 copy-start.1
where the time goes:
time: 255 us; the launch traced here: 253 us
  starting transfers between devices  86.3 us (34%)
  local copies, waits for them, and re-layouts  74.4 us (29%)
  waiting for transfers between devices  42.9 us (17%)
  other arithmetic  26.1 us (10%)
  matrix products  21.5 us (8%)
    ppermute x16, starting transfers between devices, swapped(): return lax.ppermute(block, axis, route)  86.3 us
    ppermute x16, waiting for transfers between devices, swapped(): return lax.ppermute(block, axis, route)  42.9 us
    mul x14, local copies, waits for them, and re-layouts, place_rows(): source[:, None] * selector[None, :, :, None]  27.8 us
    unnamed x98, local copies, waits for them, and re-layouts  13.4 us
    another operation x4, local copies, waits for them, and re-layouts, pick_rows(): source.reshape(length // dilation, dilation, head_count, head_size)  6.5 us
    reduce_sum x6, local copies, waits for them, and re-layouts, pick_rows(): return jnp.sum(grouped * selector[None, :, :, None], axis=1)  5.9 us
    reduce_sum x2, other arithmetic, pick_rows(): return jnp.sum(grouped * selector[None, :, :, None], axis=1)  5.71 us
    dot_general x2, matrix products, forward_level(): jnp.einsum('hmn,nhc->mhc', powered.astype(jnp.bfloat16), values_in, prefe...  5.42 us
  transfers between devices with their start and end apart: 16, of which 10 were waited for; matrix products, arithmetic and copies ran while one was open for 18% of the time, Pallas kernels for 0%

commit v1 on v0

v1 whole, which is shorter than its diff:
```python
import jax
import jax.numpy as jnp
from jax import lax
from jax.experimental import pallas as pl
from jax.experimental.pallas import tpu as pltpu
from jax.sharding import PartitionSpec as P

MESH = pl.DeviceIdType.MESH
HEADS = 10
DH = 128
TOK = 256
HALF = TOK // 2
WIDTH = HEADS * DH
GROUP = 16
ZGROUPS = 8
FACTOR = DH**-0.5
SCALE2 = FACTOR * 1.4426950408889634
LOW = -1e30
F32 = jnp.float32
BF16 = jnp.bfloat16

NN = (((1,), (0,)), ((), ()))
NT = (((1,), (1,)), ((), ()))
TN = (((0,), (0,)), ((), ()))


def mm(a, b, dims):
    return lax.dot_general(a, b, dims, preferred_element_type=F32)


def iota(shape, dim):
    return lax.broadcasted_iota(jnp.int32, shape, dim)


def split(x):
    high = x.astype(BF16)
    return high, (x - high.astype(F32)).astype(BF16)


def kernel(
    off, q_hbm, k_hbm, v_hbm, g_hbm, oq, ok, ov,
    x, px, pr, qr, sb, pb, sc, pc, tt, ts, rs, rb, lx, lr, acc, ls, ws, wx, w2, qp, wd,
    ld_sem, px_send, px_recv, p1_send, p1_recv, c1_send, c1_recv,
    p2_send, p2_recv, c2_send, c2_recv, p3_send, p3_recv, lx_send, lx_recv,
):
    me = lax.axis_index("ctx")
    core = lax.rem(me, 2)
    z = lax.rem(lax.div(me, 2), 16)
    y = lax.rem(lax.div(me, 32), 4)
    base = lax.div(me, 128) * 128
    zg = lax.div(z, 2)
    zl = lax.rem(z, 2)
    low = zl * 2 + core
    m = y * 4 + low
    mine = (lax.rem(low, 2) * 2 + lax.div(low, 2)) * 4 + y
    owner = mine < HEADS

    def member(j):
        return (base + lax.div(j, 4) * 32 + (zg * 2 + lax.rem(lax.div(j, 2), 2)) * 2 + lax.rem(j, 2),)

    def zpeer(g):
        return (base + y * 32 + (g * 2 + zl) * 2 + core,)

    def owner_of(h):
        k = lax.div(h, 4)
        return lax.rem(h, 4) * 4 + lax.rem(k, 2) * 2 + lax.div(k, 2)

    partner = (me + 1 - 2 * core,)

    def remote(src, dst, send, recv, device):
        return pltpu.make_async_remote_copy(
            src_ref=src, dst_ref=dst, send_sem=send, recv_sem=recv, device_id=device, device_id_type=MESH
        )

    loads = [
        pltpu.make_async_copy(ref, x.at[i], ld_sem.at[i]) for i, ref in enumerate((q_hbm, k_hbm, v_hbm, g_hbm))
    ]
    for load in loads:
        load.start()

    barrier = pltpu.get_barrier_semaphore()

    @pl.loop(1, GROUP)
    def _(d):
        pl.semaphore_signal(barrier, inc=1, device_id=member(lax.rem(m + d, GROUP)), device_id_type=MESH)

    @pl.loop(1, ZGROUPS)
    def _(d):
        pl.semaphore_signal(barrier, inc=1, device_id=zpeer(lax.rem(zg + d, ZGROUPS)), device_id_type=MESH)

    lane_head = lax.div(iota((8, WIDTH), 1), DH)
    off_lane = jnp.zeros((8, WIDTH), jnp.int32)
    row16 = iota((16, TOK), 0)
    off0 = jnp.zeros((16, TOK), jnp.int32)
    off1 = jnp.zeros((16, TOK), jnp.int32)
    for h in range(HEADS):
        off_lane = jnp.where(lane_head == h, off[0, h], off_lane)
        off0 = jnp.where(row16 == h, off[0, h], off0)
        off1 = jnp.where(row16 == h, off[1, h], off1)
    lane16 = iota((16, TOK), 1)
    sel_wide = (lane16 == off1).astype(F32).astype(BF16)
    row_in_pair = lax.rem(off1, 2) == off0
    key_in_pair = lax.rem(lane16, 2) == off0
    both = jnp.logical_and(row_in_pair, key_in_pair)
    weight_wide = jnp.where(both, 2.0, 1.0)
    block = lax.div(iota((16, WIDTH), 1), DH) == iota((16, WIDTH), 0)
    perm_row = iota((TOK, TOK), 0)
    perm_to = jnp.where(perm_row < HALF, 2 * perm_row, 2 * perm_row - (TOK - 1))
    perm = (iota((TOK, TOK), 1) == perm_to).astype(F32).astype(BF16)
    off_wide = off_lane[0:1, :] > 0

    sb[...] = jnp.zeros_like(sb)
    sc[...] = jnp.zeros_like(sc)
    rb[...] = jnp.zeros_like(rb)
    rs[...] = jnp.zeros_like(rs)
    ls[...] = jnp.zeros_like(ls)

    for i in range(4):
        loads[i].wait()
        picked = jnp.where(block, mm(sel_wide, x[i], NN), 0.0)
        qr[i] = picked.astype(BF16)
        for h in range(HEADS):
            sb[8 * h + i : 8 * h + i + 1, :] = picked[h : h + 1, h * DH : (h + 1) * DH]
    for i in range(4):
        parts = mm(perm, x[i], NN)
        px[i] = jnp.where(off_wide, parts[HALF:], parts[:HALF]).astype(BF16)

    pl.semaphore_wait(barrier, GROUP + ZGROUPS - 2)

    def rows_of(j):
        return pl.ds(pl.multiple_of(8 * j, 8), 8)

    def to_owner(src, dst, send, recv, h):
        return remote(src.at[rows_of(h)], dst.at[rows_of(m)], send.at[h], recv, member(owner_of(h)))

    def send_to_owners(src, dst, send, recv):
        @pl.loop(0, HEADS)
        def _(h):
            @pl.when(owner_of(h) != m)
            def _():
                to_owner(src, dst, send, recv, h).start()

            @pl.when(owner_of(h) == m)
            def _():
                pltpu.make_async_copy(src.at[rows_of(h)], dst.at[rows_of(m)], recv).start()

    def wait_sent(src, dst, send, recv):
        @pl.loop(0, HEADS)
        def _(h):
            @pl.when(owner_of(h) != m)
            def _():
                to_owner(src, dst, send, recv, h).wait_send()

    pair_copies = [remote(px.at[i], pr.at[i], px_send.at[i], px_recv.at[i], partner) for i in range(4)]
    pair_copies[1].start()
    pair_copies[2].start()
    send_to_owners(sb, pb, p1_send, p1_recv)
    pair_copies[0].start()
    pair_copies[3].start()

    s_own = mm(qr[0], x[1], NT) * SCALE2
    x_own = mm(qr[3], x[2], NT)
    pair_copies[1].wait_recv()
    pair_copies[2].wait_recv()
    s_cross = jnp.where(row_in_pair[:, :HALF], mm(qr[0], pr[1], NT) * SCALE2, LOW)
    x_cross = mm(qr[3], pr[2], NT)
    peak = jnp.maximum(jnp.max(s_own, 1, keepdims=True), jnp.max(s_cross, 1, keepdims=True))
    e_own = jnp.exp2(s_own - peak) * weight_wide
    e_cross = jnp.exp2(s_cross - peak)
    total = jnp.sum(e_own, 1, keepdims=True) + jnp.sum(e_cross, 1, keepdims=True)
    blend = jnp.sum(e_own * x_own, 1, keepdims=True) + jnp.sum(e_cross * x_cross, 1, keepdims=True)
    lane128 = iota((16, DH), 1)
    wide_stats = jnp.where(lane128 == 0, peak + jnp.log2(total), jnp.where(lane128 == 1, blend / total, 0.0))
    for h in range(HEADS):
        sc[8 * h : 8 * h + 1, :] = wide_stats[h : h + 1, :]
    send_to_owners(sc, pc, c1_send, c1_recv)
    ws[0] = s_own
    ws[1] = x_own
    wx[0] = s_cross
    wx[1] = x_cross

    def to_zpeer(src, send, recv, d):
        return remote(src.at[zg], src.at[zg], send.at[d], recv, zpeer(lax.rem(zg + d, ZGROUPS)))

    @pl.when(owner)
    def _():
        pltpu.make_async_copy(pb, pb, p1_recv).wait()
        for i in range(4):
            tt[zg, i] = pb[pl.ds(i, GROUP, stride=8), :].astype(BF16)

        @pl.loop(1, ZGROUPS)
        def _(d):
            to_zpeer(tt, p2_send, p2_recv, d).start()

    @pl.when(owner)
    def _():
        pltpu.make_async_copy(pc, pc, c1_recv).wait()
        ts[zg] = pc[pl.ds(0, GROUP, stride=8), :]

        @pl.loop(1, ZGROUPS)
        def _(d):
            to_zpeer(ts, c2_send, c2_recv, d).start()

    pair_copies[0].wait_recv()
    pair_copies[3].wait_recv()
    lane_pair = iota((16, HALF), 1)
    sel_pair = jnp.logical_and(row_in_pair[:, :HALF], lane_pair == lax.div(off1[:, :HALF], 2))
    sel_pair = sel_pair.astype(F32).astype(BF16)
    qp[0] = jnp.where(block, mm(sel_pair, pr[0], NN), 0.0).astype(BF16)
    qp[1] = jnp.where(block, mm(sel_pair, pr[3], NN), 0.0).astype(BF16)
    w2[0] = jnp.where(both, mm(qp[0], x[1], NT) * SCALE2, LOW)
    w2[1] = mm(qp[1], x[2], NT)

    lane_row = iota((1, TOK), 1)
    parity_lane = lax.rem(lane_row, 2)
    parity_row = lax.rem(iota((TOK, HALF), 0), 2)
    parity_row2 = lax.rem(iota((TOK, TOK), 0), 2)

    @pl.loop(0, HEADS)
    def _(h):
        hs = pl.ds(pl.multiple_of(h * DH, DH), DH)
        qh = x[0, :, hs]
        gh = x[3, :, hs]
        kh = x[1, :, hs]
        vh = x[2, :, hs]
        kx = pr[1, :, hs]
        vx = pr[2, :, hs]
        chosen = parity_lane == off[0, h]
        keep = jnp.where(lane_row == off[1, h], 0.0, 1.0)
        weight = jnp.where(jnp.logical_and(parity_row2 == off[0, h], chosen), 2.0, 1.0)
        s0 = mm(kh, qh, NT) * SCALE2
        s1 = mm(kx, qh, NT) * SCALE2 + jnp.where(chosen, 0.0, LOW)
        x0 = mm(vh, gh, NT)
        x1 = mm(vx, gh, NT)
        top = jnp.maximum(jnp.max(s0, 0, keepdims=True), jnp.max(s1, 0, keepdims=True))
        e0 = jnp.exp2(s0 - top) * weight
        e1 = jnp.exp2(s1 - top)
        tot = jnp.sum(e0, 0, keepdims=True) + jnp.sum(e1, 0, keepdims=True)
        num = jnp.sum(e0 * x0, 0, keepdims=True) + jnp.sum(e1 * x1, 0, keepdims=True)
        inv = 1.0 / tot
        delta = num * inv
        ls[0, pl.ds(h, 1), :] = jnp.where(keep > 0, top + jnp.log2(tot), -LOW)
        ls[1, pl.ds(h, 1), :] = delta
        gain = inv * keep
        p0 = e0 * gain
        p1 = e1 * gain
        d0 = ((p0 * FACTOR) * (x0 - delta)).astype(BF16)
        d1 = ((p1 * FACTOR) * (x1 - delta)).astype(BF16)
        acc[2, :, hs] = mm(p0.astype(BF16), gh, NN)
        acc[1, :, hs] = mm(d0, qh, NN)
        acc[0, :, hs] = mm(d0, kh, TN) + mm(d1, kx, TN)

    perm_t = jnp.where(iota((TOK, TOK), 1) < HALF, 2 * iota((TOK, TOK), 1), 2 * iota((TOK, TOK), 1) - (TOK - 1))
    perm_t = (iota((TOK, TOK), 0) == perm_t).astype(F32).astype(BF16)
    for i in range(2):
        value = ls[i]
        high, rest = split(value)
        mid, least = split(value - high.astype(F32))
        moved = mm(high, perm_t, NN) + (mm(mid, perm_t, NN) + mm(least, perm_t, NN))
        lx[i] = jnp.where(off0[:, :HALF] > 0, moved[:, HALF:], moved[:, :HALF])
    stat_copy = remote(lx, lr, lx_send, lx_recv, partner)
    stat_copy.start()
    stat_copy.wait_recv()

    @pl.loop(0, HEADS)
    def _(h):
        hs = pl.ds(pl.multiple_of(h * DH, DH), DH)
        kh = x[1, :, hs]
        vh = x[2, :, hs]
        qx = pr[0, :, hs]
        gx = pr[3, :, hs]
        lse = lr[0, pl.ds(h, 1), :]
        delta = lr[1, pl.ds(h, 1), :]
        s2 = mm(kh, qx, NT) * SCALE2
        x2 = mm(vh, gx, NT)
        p2 = jnp.exp2(jnp.where(parity_row == off[0, h], s2 - lse, LOW))
        d2 = ((p2 * FACTOR) * (x2 - delta)).astype(BF16)
        acc[2, :, hs] += mm(p2.astype(BF16), gx, NN)
        acc[1, :, hs] += mm(d2, qx, NN)

    def to_member(d):
        j = lax.rem(m + d, GROUP)
        return remote(rs.at[rows_of(j)], rb.at[rows_of(mine)], p3_send.at[d], p3_recv, member(j))

    @pl.when(owner)
    def _():
        seven = pl.ds(0, ZGROUPS - 1)
        pltpu.make_async_copy(tt.at[seven], tt.at[seven], p2_recv).wait()
        pltpu.make_async_copy(ts.at[seven], ts.at[seven], c2_recv).wait()
        qw, kw, vw, gw = [tt[:, i].reshape(128, DH) for i in range(4)]
        stat = ts[...].reshape(128, DH)
        lse_lp, delta_lp = stat[:, 0:1], stat[:, 1:2]
        s = mm(qw, kw, NT) * SCALE2
        xx = mm(gw, vw, NT)
        top = jnp.max(s, 1, keepdims=True)
        e = jnp.exp2(s - top)
        tot = jnp.sum(e, 1, keepdims=True)
        num = jnp.sum(e * xx, 1, keepdims=True)
        peak = jnp.maximum(top, lse_lp)
        c_w = jnp.exp2(top - peak)
        c_lp = jnp.exp2(lse_lp - peak)
        all_tot = tot * c_w + c_lp
        lse = peak + jnp.log2(all_tot)
        delta = (num * c_w + delta_lp * c_lp) / all_tot
        p = e * (c_w / all_tot)
        ds = ((p * FACTOR) * (xx - delta)).astype(BF16)
        wd[0] = mm(ds, kw, NN)
        wd[1] = mm(ds, qw, TN)
        wd[2] = mm(p.astype(BF16), gw, TN)
        lane = iota((128, DH), 1)
        both_stats = jnp.where(lane == 0, lse, jnp.where(lane == 1, delta, 0.0))
        wd[3] = both_stats
        own = pl.ds(pl.multiple_of(zg * GROUP, GROUP), GROUP)
        for i in range(4):
            rs[pl.ds(i, GROUP, stride=8), :] = wd[i, own, :]
        stats16 = wd[3, own, :]
        even = lax.rem(iota((GROUP, DH), 0), 2) == 0
        swapped = jnp.where(even, pltpu.roll(stats16, GROUP - 1, 0), pltpu.roll(stats16, 1, 0))
        rs[pl.ds(4, GROUP, stride=8), :] = swapped

        @pl.loop(1, GROUP)
        def _(d):
            to_member(d).start()

        pltpu.make_async_copy(rs.at[rows_of(m)], rb.at[rows_of(mine)], p3_recv).start()

    got = pl.ds(0, 8 * HEADS)
    pltpu.make_async_copy(rb.at[got], rb.at[got], p3_recv).wait()

    own_stat = rb[pl.ds(3, 16, stride=8), :]
    far_stat = rb[pl.ds(4, 16, stride=8), :]
    lse_r, delta_r = own_stat[:, 0:1], own_stat[:, 1:2]
    lse_f, delta_f = far_stat[:, 0:1], far_stat[:, 1:2]
    p_own = jnp.exp2(ws[0] - lse_r) * weight_wide
    d_own = ((p_own * FACTOR) * (ws[1] - delta_r)).astype(BF16)
    p_cross = jnp.exp2(wx[0] - lse_r)
    d_cross = ((p_cross * FACTOR) * (wx[1] - delta_r)).astype(BF16)
    p_far = jnp.exp2(w2[0] - lse_f)
    d_far = ((p_far * FACTOR) * (w2[1] - delta_f)).astype(BF16)

    def spread(i):
        row = rb[pl.ds(i, 16, stride=8), :]
        return jnp.where(block, jnp.concatenate([row] * HEADS, axis=1), 0.0)

    dq_row = jnp.where(block, mm(d_own, x[1], NN) + mm(d_cross, pr[1], NN), 0.0) + spread(0)
    sel = sel_wide
    fixes = (
        (oq, 0, jnp.concatenate([sel, sel], 0), jnp.concatenate(split(dq_row), 0)),
        (ok, 1, jnp.concatenate([d_own, d_far, sel, sel], 0), jnp.concatenate([qr[0], qp[0], *split(spread(1))], 0)),
        (
            ov,
            2,
            jnp.concatenate([p_own.astype(BF16), p_far.astype(BF16), sel, sel], 0),
            jnp.concatenate([qr[3], qp[1], *split(spread(2))], 0),
        ),
    )
    for ref, i, left, right in fixes:
        ref[...] = (acc[i] + mm(left, right, TN)).astype(BF16)

    for copy in pair_copies:
        copy.wait_send()
    stat_copy.wait_send()
    wait_sent(sb, pb, p1_send, p1_recv)
    wait_sent(sc, pc, c1_send, c1_recv)

    @pl.when(owner)
    def _():
        @pl.loop(1, ZGROUPS)
        def _(d):
            to_zpeer(tt, p2_send, p2_recv, d).wait_send()
            to_zpeer(ts, c2_send, c2_recv, d).wait_send()

        @pl.loop(1, GROUP)
        def _(d):
            to_member(d).wait_send()


def on_device(query, key, value, grad_out, offsets):
    shape = jax.ShapeDtypeStruct((TOK, WIDTH), BF16)
    vmem = pltpu.VMEM
    dma = pltpu.SemaphoreType.DMA
    return pl.pallas_call(
        kernel,
        out_shape=(shape, shape, shape),
        in_specs=[pl.BlockSpec(memory_space=pltpu.SMEM)] + [pl.BlockSpec(memory_space=pl.ANY)] * 4,
        out_specs=(pl.BlockSpec(memory_space=vmem),) * 3,
        scratch_shapes=[
            vmem((4, TOK, WIDTH), BF16),
            vmem((4, HALF, WIDTH), BF16),
            vmem((4, HALF, WIDTH), BF16),
            vmem((4, 16, WIDTH), BF16),
            vmem((8 * HEADS, DH), F32),
            vmem((8 * GROUP, DH), F32),
            vmem((8 * HEADS, DH), F32),
            vmem((8 * GROUP, DH), F32),
            vmem((ZGROUPS, 4, GROUP, DH), BF16),
            vmem((ZGROUPS, GROUP, DH), F32),
            vmem((8 * GROUP, DH), F32),
            vmem((8 * 16, DH), F32),
            vmem((2, 16, HALF), F32),
            vmem((2, 16, HALF), F32),
            vmem((3, TOK, WIDTH), F32),
            vmem((2, 16, TOK), F32),
            vmem((2, 16, TOK), F32),
            vmem((2, 16, HALF), F32),
            vmem((2, 16, TOK), F32),
            vmem((2, 16, WIDTH), BF16),
            vmem((4, 128, DH), F32),
            dma((4,)),
            dma((4,)),
            dma((4,)),
            dma((HEADS,)),
            dma(()),
            dma((HEADS,)),
            dma(()),
            dma((ZGROUPS,)),
            dma(()),
            dma((ZGROUPS,)),
            dma(()),
            dma((GROUP,)),
            dma(()),
            dma(()),
            dma(()),
        ],
        compiler_params=pltpu.CompilerParams(collective_id=0, has_side_effects=True, vmem_limit_bytes=48 * 1024 * 1024),
    )(offsets, query, key, value, grad_out)


def solution(mesh):
    placed = (P("ctx", None),) * 4 + (P(),)
    return jax.shard_map(
        on_device, mesh=mesh, in_specs=placed, out_specs=(P("ctx", None),) * 3, check_vma=False
    )
```

time: 255 us -> 50.2 us (0.20)
  starting transfers between devices: 86.3 us -> 0 us
  local copies, waits for them, and re-layouts: 74.4 us -> 7.53 us
  waiting for transfers between devices: 42.9 us -> 0 us
  Pallas kernels: 0 us -> 41.7 us
  other arithmetic: 26.1 us -> 0 us
  matrix products: 21.5 us -> 0 us
    ppermute x16 -> x0, starting transfers between devices: 86.3 us -> none  [swapped(): return lax.ppermute(block, axis, route)]
    ppermute x16 -> x0, waiting for transfers between devices: 42.9 us -> none  [swapped(): return lax.ppermute(block, axis, route)]
    pallas_call x0 -> x1, Pallas kernels: none -> 41.7 us  [on_device(): pl.pallas_call(kernel, out_shape=(shape, shape, shape), in_specs=[pl.Bloc...]
    mul x19 -> x0, local copies, waits for them, and re-layouts: 32.4 us -> none  [the longest x14 27.8 us: place_rows(): source[:, None] * selector[None, :, :, None]]
    dot_general x12 -> x0, matrix products: 21.5 us -> none  [the longest x2 5.42 us: forward_level(): jnp.einsum('hmn,nhc->mhc', powered.astype(jnp.bfloat16), values_in, prefe...]
    reduce_sum x6 -> x0, other arithmetic: 12 us -> none  [the longest x2 5.71 us: pick_rows(): return jnp.sum(grouped * selector[None, :, :, None], axis=1)]
    reduce_sum x10 -> x0, local copies, waits for them, and re-layouts: 9.29 us -> none  [the longest x6 5.9 us: pick_rows(): return jnp.sum(grouped * selector[None, :, :, None], axis=1)]
    another operation x4 -> x0, local copies, waits for them, and re-layouts: 6.5 us -> none  [pick_rows(): source.reshape(length // dilation, dilation, head_count, head_size)]
  transfers between devices with their start and end apart: 16 -> 0, of which waited for: 10 -> 0; matrix products, arithmetic and copies ran while one was open for 18% -> 0% of each run, Pallas kernels for 0% -> 0%
where the time goes in v1:
time: 50.2 us; the launch traced here: 49.9 us
  Pallas kernels  41.7 us (83%)
  local copies, waits for them, and re-layouts  7.53 us (15%)
  between operations  0.65 us (1%)
    pallas_call x1, Pallas kernels, on_device(): pl.pallas_call(kernel, out_shape=(shape, shape, shape), in_specs=[pl.Bloc...  41.7 us
    unnamed x13, local copies, waits for them, and re-layouts  7.53 us

profile of v1, /device:TPU:1, one launch (start us, length us, event | category | flops | bytes accessed | tf_op | source)
XLA Modules:
  0.0 49.9 jit_solution(7378935687083112580)
XLA Ops:
  0.6 0.0 copy-start
  0.6 1.1 %copy-done = bf16[256,1280]{1,0:T(8,128)(2,1)S(1)} copy-done((bf16[256,1280]{1,0:T(8,128)(2,1)S(1)}, bf16[256,1280]{1,0:T(8,128)(2,1)}, u32[]{:S(2)}) %copy-start) | copy-done | bytes 655384
  1.7 0.0 copy-start.1
  1.7 1.1 %copy-done.1 = bf16[256,1280]{1,0:T(8,128)(2,1)S(1)} copy-done((bf16[256,1280]{1,0:T(8,128)(2,1)S(1)}, bf16[256,1280]{1,0:T(8,128)(2,1)}, u32[]{:S(2)}) %copy-start.1) | copy-done | bytes 655384
  2.8 0.0 copy-start.2
  2.8 1.1 %copy-done.2 = bf16[256,1280]{1,0:T(8,128)(2,1)S(1)} copy-done((bf16[256,1280]{1,0:T(8,128)(2,1)S(1)}, bf16[256,1280]{1,0:T(8,128)(2,1)}, u32[]{:S(2)}) %copy-start.2) | copy-done | bytes 655384
  3.9 0.0 copy-start.3
  3.9 1.1 %copy-done.3 = bf16[256,1280]{1,0:T(8,128)(2,1)S(1)} copy-done((bf16[256,1280]{1,0:T(8,128)(2,1)S(1)}, bf16[256,1280]{1,0:T(8,128)(2,1)}, u32[]{:S(2)}) %copy-start.3) | copy-done | bytes 655384
  5.0 0.0 copy-start.4
  5.0 0.7 %copy-done.4 = s32[2,10]{1,0:T(2,128)S(1)} copy-done((s32[2,10]{1,0:T(2,128)S(1)}, s32[2,10]{1,0:T(2,128)}, u32[]{:S(2)}) %copy-start.4) | copy-done | bytes 104
  5.7 41.7 %shard_map.76 = (bf16[256,1280]{1,0:T(8,128)(2,1)S(1)}, bf16[256,1280]{1,0:T(8,128)(2,1)S(1)}, bf16[256,1280]{1,0:T(8,128)(2,1)S(1)}) custom-call(s32[2,10]{1,0:T(2,128)S(1)} %copy-done.4, bf16[256,1280]{1,0:T(8,128)(2,1)S(1)} %copy-done, bf16[256,1280]{1,0:T(8,128)(2,1)S(1)} %copy-done.1, bf16[256,1280]{1,0:T(8,128)(2,1)S(1)} %copy-done.2, ...), custom_call_target="tpu_custom_call" | custom-call | tf_op jit(solution)/shard_map/pallas_call | solution.py:382
  47.3 0.8 %copy.11 = bf16[256,1280]{1,0:T(8,128)(2,1)} copy(bf16[256,1280]{1,0:T(8,128)(2,1)S(1)} %get-tuple-element.6) | data formatting | bytes 1310720
  48.2 0.8 %copy.12 = bf16[256,1280]{1,0:T(8,128)(2,1)} copy(bf16[256,1280]{1,0:T(8,128)(2,1)S(1)} %get-tuple-element.7) | data formatting | bytes 1310720
  49.0 0.8 %copy.13 = bf16[256,1280]{1,0:T(8,128)(2,1)} copy(bf16[256,1280]{1,0:T(8,128)(2,1)S(1)} %get-tuple-element.8) | data formatting | bytes 1310720
Async XLA Ops:
  0.6 1.1 %copy-start = (bf16[256,1280]{1,0:T(8,128)(2,1)S(1)}, bf16[256,1280]{1,0:T(8,128)(2,1)}, u32[]{:S(2)}) copy-start(bf16[256,1280]{1,0:T(8,128)(2,1)} %q_hbm.1) | copy-start | bytes 1966084
  1.7 1.1 %copy-start.1 = (bf16[256,1280]{1,0:T(8,128)(2,1)S(1)}, bf16[256,1280]{1,0:T(8,128)(2,1)}, u32[]{:S(2)}) copy-start(bf16[256,1280]{1,0:T(8,128)(2,1)} %k_hbm.1) | copy-start | bytes 1966084
  2.8 1.1 %copy-start.2 = (bf16[256,1280]{1,0:T(8,128)(2,1)S(1)}, bf16[256,1280]{1,0:T(8,128)(2,1)}, u32[]{:S(2)}) copy-start(bf16[256,1280]{1,0:T(8,128)(2,1)} %v_hbm.1) | copy-start | bytes 1966084
  3.9 1.1 %copy-start.3 = (bf16[256,1280]{1,0:T(8,128)(2,1)S(1)}, bf16[256,1280]{1,0:T(8,128)(2,1)}, u32[]{:S(2)}) copy-start(bf16[256,1280]{1,0:T(8,128)(2,1)} %g_hbm.1) | copy-start | bytes 1966084
  5.0 0.7 %copy-start.4 = (s32[2,10]{1,0:T(2,128)S(1)}, s32[2,10]{1,0:T(2,128)}, u32[]{:S(2)}) copy-start(s32[2,10]{1,0:T(2,128)} %off.1) | copy-start | bytes 244

commit v2 on v1

v2 whole, which is shorter than its diff:
```python
import jax
import jax.numpy as jnp
from jax import lax
from jax.experimental import pallas as pl
from jax.experimental.pallas import tpu as pltpu
from jax.sharding import PartitionSpec as P

MESH = pl.DeviceIdType.MESH
HEADS = 10
DH = 128
TOK = 256
HALF = TOK // 2
WIDTH = HEADS * DH
GROUP = 16
ZGROUPS = 8
FACTOR = DH**-0.5
SCALE2 = FACTOR * 1.4426950408889634
LOW = -1e30
UNROLL = 2
EARLY = 1
MIDDLE = 2
F32 = jnp.float32
BF16 = jnp.bfloat16

NN = (((1,), (0,)), ((), ()))
NT = (((1,), (1,)), ((), ()))
TN = (((0,), (0,)), ((), ()))


def mm(a, b, dims):
    return lax.dot_general(a, b, dims, preferred_element_type=F32)


def iota(shape, dim):
    return lax.broadcasted_iota(jnp.int32, shape, dim)


def split(x):
    high = x.astype(BF16)
    return high, (x - high.astype(F32)).astype(BF16)


def kernel(
    off_hbm, q_hbm, k_hbm, v_hbm, g_hbm, oq, ok, ov,
    x, px, pr, qr, sb, pb, sc, pc, tt, ts, rs, rb, lx, lr, acc, ls, ws, wx, w2, qp, wd, off,
    ld_sem, off_sem, ready, px_send, px_recv, p1_send, p1_recv, c1_send, c1_recv,
    p2_send, p2_recv, c2_send, c2_recv, p3_send, p3_recv, lx_send, lx_recv,
):
    me = lax.axis_index("ctx")
    core = lax.rem(me, 2)
    z = lax.rem(lax.div(me, 2), 16)
    y = lax.rem(lax.div(me, 32), 4)
    base = lax.div(me, 128) * 128
    zg = lax.div(z, 2)
    zl = lax.rem(z, 2)
    low = zl * 2 + core
    m = y * 4 + low
    mine = (lax.rem(low, 2) * 2 + lax.div(low, 2)) * 4 + y
    owner = mine < HEADS

    def member(j):
        return (base + lax.div(j, 4) * 32 + (zg * 2 + lax.rem(lax.div(j, 2), 2)) * 2 + lax.rem(j, 2),)

    def zpeer(g):
        return (base + y * 32 + (g * 2 + zl) * 2 + core,)

    def owner_of(h):
        k = lax.div(h, 4)
        return lax.rem(h, 4) * 4 + lax.rem(k, 2) * 2 + lax.div(k, 2)

    partner = (me + 1 - 2 * core,)

    def remote(src, dst, send, recv, device):
        return pltpu.make_async_remote_copy(
            src_ref=src, dst_ref=dst, send_sem=send, recv_sem=recv, device_id=device, device_id_type=MESH
        )

    barrier = pltpu.get_barrier_semaphore()
    right = zpeer(lax.rem(zg + 1, ZGROUPS))
    left = zpeer(lax.rem(zg + ZGROUPS - 1, ZGROUPS))
    pl.semaphore_signal(barrier, inc=1, device_id=right, device_id_type=MESH)
    pl.semaphore_signal(barrier, inc=1, device_id=left, device_id_type=MESH)

    @pl.loop(1, GROUP)
    def _(d):
        pl.semaphore_signal(barrier, inc=1, device_id=member(lax.rem(m + d, GROUP)), device_id_type=MESH)

    off_load = pltpu.make_async_copy(off_hbm, off, off_sem)
    off_load.start()
    loads = [
        pltpu.make_async_copy(ref, x.at[i], ld_sem.at[i]) for i, ref in enumerate((q_hbm, k_hbm, v_hbm, g_hbm))
    ]
    for i in (1, 2, 0, 3):
        loads[i].start()

    def pass_on(stage):
        @pl.when(owner)
        def _():
            if stage > 0:
                pl.semaphore_wait(ready.at[2 * stage - 2], 1)
                pl.semaphore_wait(ready.at[2 * stage - 1], 1)
            if stage < 3:
                pl.semaphore_signal(ready.at[2 * stage], inc=1, device_id=right, device_id_type=MESH)
                pl.semaphore_signal(ready.at[2 * stage + 1], inc=1, device_id=left, device_id_type=MESH)

    sb[...] = jnp.zeros_like(sb)
    sc[...] = jnp.zeros_like(sc)
    rb[...] = jnp.zeros_like(rb)
    rs[...] = jnp.zeros_like(rs)
    ls[...] = jnp.zeros_like(ls)
    perm_row = iota((TOK, TOK), 0)
    perm_to = jnp.where(perm_row < HALF, 2 * perm_row, 2 * perm_row - (TOK - 1))
    perm = (iota((TOK, TOK), 1) == perm_to).astype(F32).astype(BF16)
    block = lax.div(iota((16, WIDTH), 1), DH) == iota((16, WIDTH), 0)
    lane_head = lax.div(iota((8, WIDTH), 1), DH)
    row16 = iota((16, TOK), 0)
    lane16 = iota((16, TOK), 1)

    off_load.wait()
    off_lane = jnp.zeros((8, WIDTH), jnp.int32)
    off0 = jnp.zeros((16, TOK), jnp.int32)
    off1 = jnp.zeros((16, TOK), jnp.int32)
    for h in range(HEADS):
        off_lane = jnp.where(lane_head == h, off[0, h], off_lane)
        off0 = jnp.where(row16 == h, off[0, h], off0)
        off1 = jnp.where(row16 == h, off[1, h], off1)
    sel_wide = (lane16 == off1).astype(F32).astype(BF16)
    row_in_pair = lax.rem(off1, 2) == off0
    key_in_pair = lax.rem(lane16, 2) == off0
    both = jnp.logical_and(row_in_pair, key_in_pair)
    weight_wide = jnp.where(both, 2.0, 1.0)
    off_wide = off_lane[0:1, :] > 0

    def pack_pair(i):
        parts = mm(perm, x[i], NN)
        px[i] = jnp.where(off_wide, parts[HALF:], parts[:HALF]).astype(BF16)

    pair_copies = [remote(px.at[i], pr.at[i], px_send.at[i], px_recv.at[i], partner) for i in range(4)]

    def rows_of(j):
        return pl.ds(pl.multiple_of(8 * j, 8), 8)

    def to_owner(src, dst, send, recv, h):
        return remote(src.at[rows_of(h)], dst.at[rows_of(m)], send.at[h], recv, member(owner_of(h)))

    def send_to_owners(src, dst, send, recv):
        @pl.loop(0, HEADS)
        def _(h):
            @pl.when(owner_of(h) != m)
            def _():
                to_owner(src, dst, send, recv, h).start()

            @pl.when(owner_of(h) == m)
            def _():
                pltpu.make_async_copy(src.at[rows_of(h)], dst.at[rows_of(m)], recv).start()

    def wait_sent(src, dst, send, recv):
        @pl.loop(0, HEADS)
        def _(h):
            @pl.when(owner_of(h) != m)
            def _():
                to_owner(src, dst, send, recv, h).wait_send()

    loads[1].wait()
    pack_pair(1)
    loads[2].wait()
    pack_pair(2)

    pl.semaphore_wait(barrier, GROUP + 1)
    pass_on(0)
    pair_copies[1].start()
    pair_copies[2].start()

    loads[0].wait()
    loads[3].wait()
    for i in range(4):
        picked = jnp.where(block, mm(sel_wide, x[i], NN), 0.0)
        qr[i] = picked.astype(BF16)
        for h in range(HEADS):
            sb[8 * h + i : 8 * h + i + 1, :] = picked[h : h + 1, h * DH : (h + 1) * DH]
    send_to_owners(sb, pb, p1_send, p1_recv)

    s_own = mm(qr[0], x[1], NT) * SCALE2
    x_own = mm(qr[3], x[2], NT)
    pair_copies[1].wait_recv()
    pair_copies[2].wait_recv()
    s_cross = jnp.where(row_in_pair[:, :HALF], mm(qr[0], pr[1], NT) * SCALE2, LOW)
    x_cross = mm(qr[3], pr[2], NT)
    peak = jnp.maximum(jnp.max(s_own, 1, keepdims=True), jnp.max(s_cross, 1, keepdims=True))
    e_own = jnp.exp2(s_own - peak) * weight_wide
    e_cross = jnp.exp2(s_cross - peak)
    total = jnp.sum(e_own, 1, keepdims=True) + jnp.sum(e_cross, 1, keepdims=True)
    blend = jnp.sum(e_own * x_own, 1, keepdims=True) + jnp.sum(e_cross * x_cross, 1, keepdims=True)
    lane128 = iota((16, DH), 1)
    here = lane128 == zg * GROUP + m
    wide_lse = jnp.where(here, peak + jnp.log2(total), 0.0)
    wide_delta = jnp.where(here, blend / total, 0.0)
    for h in range(HEADS):
        sc[8 * h : 8 * h + 1, :] = wide_lse[h : h + 1, :]
        sc[8 * h + 1 : 8 * h + 2, :] = wide_delta[h : h + 1, :]
    send_to_owners(sc, pc, c1_send, c1_recv)
    ws[0] = s_own
    ws[1] = x_own
    wx[0] = s_cross
    wx[1] = x_cross
    pass_on(1)
    pack_pair(0)
    pair_copies[0].start()
    pack_pair(3)
    pair_copies[3].start()
    pass_on(2)

    lane_row = iota((1, TOK), 1)
    parity_lane = lax.rem(lane_row, 2)
    parity_sub = lax.rem(iota((1, 8, TOK), 1), 2)
    parity_both = lax.rem(iota((1, 8, TOK), 2), 2)

    def total_of(a):
        return jnp.sum(jnp.sum(a, 0), 0, keepdims=True)

    def peak_of(a):
        return jnp.max(jnp.max(a, 0), 0, keepdims=True)

    def attend(h):
        hs = pl.ds(pl.multiple_of(h * DH, DH), DH)
        qh = x[0, :, hs]
        gh = x[3, :, hs]
        kh = x[1, :, hs]
        vh = x[2, :, hs]
        kx = pr[1, :, hs]
        vx = pr[2, :, hs]
        chosen = parity_lane == off[0, h]
        keep = jnp.where(lane_row == off[1, h], 0.0, 1.0)
        weight = jnp.where(jnp.logical_and(parity_sub == off[0, h], parity_both == off[0, h]), 2.0, 1.0)
        s0 = (mm(kh, qh, NT) * SCALE2).reshape(TOK // 8, 8, TOK)
        s1 = (mm(kx, qh, NT) * SCALE2 + jnp.where(chosen, 0.0, LOW)).reshape(HALF // 8, 8, TOK)
        x0 = mm(vh, gh, NT).reshape(TOK // 8, 8, TOK)
        x1 = mm(vx, gh, NT).reshape(HALF // 8, 8, TOK)
        top = jnp.maximum(peak_of(s0), peak_of(s1))
        e0 = jnp.exp2(s0 - top) * weight
        e1 = jnp.exp2(s1 - top)
        tot = total_of(e0) + total_of(e1)
        num = total_of(e0 * x0) + total_of(e1 * x1)
        inv = 1.0 / tot
        delta = num * inv
        ls[0, pl.ds(h, 1), :] = jnp.where(keep > 0, top + jnp.log2(tot), -LOW)
        ls[1, pl.ds(h, 1), :] = delta
        gain = inv * keep
        slope = gain * FACTOR
        p0 = e0 * gain
        d0 = ((e0 * slope) * (x0 - delta)).reshape(TOK, TOK).astype(BF16)
        d1 = ((e1 * slope) * (x1 - delta)).reshape(HALF, TOK).astype(BF16)
        acc[2, :, hs] = mm(p0.reshape(TOK, TOK).astype(BF16), gh, NN)
        acc[1, :, hs] = mm(d0, qh, NN)
        acc[0, :, hs] = mm(d0, kh, TN) + mm(d1, kx, TN)

    @pl.loop(0, EARLY)
    def _(j):
        for u in range(UNROLL):
            attend(j * UNROLL + u)

    def to_zpeer(src, send, recv, d):
        return remote(src.at[zg], src.at[zg], send.at[d], recv, zpeer(lax.rem(zg + d, ZGROUPS)))

    pass_on(3)

    @pl.when(owner)
    def _():
        pltpu.make_async_copy(pb, pb, p1_recv).wait()
        for i in range(4):
            tt[zg, i] = pb[pl.ds(i, GROUP, stride=8), :].astype(BF16)

        @pl.loop(1, ZGROUPS)
        def _(d):
            to_zpeer(tt, p2_send, p2_recv, d).start()

    @pl.loop(EARLY, MIDDLE)
    def _(j):
        for u in range(UNROLL):
            attend(j * UNROLL + u)

    @pl.when(owner)
    def _():
        pltpu.make_async_copy(pc, pc, c1_recv).wait()
        for i in range(2):
            ts[zg, i : i + 1, :] = jnp.sum(pc[pl.ds(i, GROUP, stride=8), :], 0, keepdims=True)

        @pl.loop(1, ZGROUPS)
        def _(d):
            to_zpeer(ts, c2_send, c2_recv, d).start()

    @pl.loop(MIDDLE, HEADS // UNROLL)
    def _(j):
        for u in range(UNROLL):
            attend(j * UNROLL + u)

    perm_t = jnp.where(iota((TOK, TOK), 1) < HALF, 2 * iota((TOK, TOK), 1), 2 * iota((TOK, TOK), 1) - (TOK - 1))
    perm_t = (iota((TOK, TOK), 0) == perm_t).astype(F32).astype(BF16)
    for i in range(2):
        value = ls[i]
        high, rest = split(value)
        mid, least = split(value - high.astype(F32))
        moved = mm(high, perm_t, NN) + (mm(mid, perm_t, NN) + mm(least, perm_t, NN))
        lx[i] = jnp.where(off0[:, :HALF] > 0, moved[:, HALF:], moved[:, :HALF])
    stat_copy = remote(lx, lr, lx_send, lx_recv, partner)
    stat_copy.start()

    pair_copies[0].wait_recv()
    pair_copies[3].wait_recv()
    lane_pair = iota((16, HALF), 1)
    sel_pair = jnp.logical_and(row_in_pair[:, :HALF], lane_pair == lax.div(off1[:, :HALF], 2))
    sel_pair = sel_pair.astype(F32).astype(BF16)
    qp[0] = jnp.where(block, mm(sel_pair, pr[0], NN), 0.0).astype(BF16)
    qp[1] = jnp.where(block, mm(sel_pair, pr[3], NN), 0.0).astype(BF16)
    w2[0] = jnp.where(both, mm(qp[0], x[1], NT) * SCALE2, LOW)
    w2[1] = mm(qp[1], x[2], NT)

    stat_copy.wait_recv()

    def cross(h):
        hs = pl.ds(pl.multiple_of(h * DH, DH), DH)
        kh = x[1, :, hs]
        vh = x[2, :, hs]
        qx = pr[0, :, hs]
        gx = pr[3, :, hs]
        lse = lr[0, pl.ds(h, 1), :]
        delta = lr[1, pl.ds(h, 1), :]
        s2 = (mm(kh, qx, NT) * SCALE2).reshape(TOK // 8, 8, HALF)
        x2 = mm(vh, gx, NT).reshape(TOK // 8, 8, HALF)
        p2 = jnp.exp2(jnp.where(parity_sub[:, :, :HALF] == off[0, h], s2 - lse, LOW))
        d2 = ((p2 * FACTOR) * (x2 - delta)).reshape(TOK, HALF).astype(BF16)
        acc[2, :, hs] += mm(p2.reshape(TOK, HALF).astype(BF16), gx, NN)
        acc[1, :, hs] += mm(d2, qx, NN)

    @pl.loop(0, HEADS // UNROLL)
    def _(j):
        for u in range(UNROLL):
            cross(j * UNROLL + u)

    def to_member(d):
        j = lax.rem(m + d, GROUP)
        return remote(rs.at[rows_of(j)], rb.at[rows_of(mine)], p3_send.at[d], p3_recv, member(j))

    @pl.when(owner)
    def _():
        seven = pl.ds(0, ZGROUPS - 1)
        pltpu.make_async_copy(tt.at[seven], tt.at[seven], p2_recv).wait()
        pltpu.make_async_copy(ts.at[seven], ts.at[seven], c2_recv).wait()
        qw, kw, vw, gw = [tt[:, i].reshape(128, DH) for i in range(4)]
        stat = jnp.sum(ts[...], 0)
        lse_lp, delta_lp = stat[0:1], stat[1:2]
        s = mm(kw, qw, NT) * SCALE2
        xx = mm(vw, gw, NT)
        top = jnp.max(s, 0, keepdims=True)
        e = jnp.exp2(s - top)
        tot = jnp.sum(e, 0, keepdims=True)
        num = jnp.sum(e * xx, 0, keepdims=True)
        peak = jnp.maximum(top, lse_lp)
        c_w = jnp.exp2(top - peak)
        c_lp = jnp.exp2(lse_lp - peak)
        all_tot = tot * c_w + c_lp
        lse = peak + jnp.log2(all_tot)
        delta = (num * c_w + delta_lp * c_lp) / all_tot
        p = e * (c_w / all_tot)
        ds = ((p * FACTOR) * (xx - delta)).astype(BF16)
        wd[0] = mm(ds, kw, TN)
        wd[1] = mm(ds, qw, NN)
        wd[2] = mm(p.astype(BF16), gw, NN)
        own = pl.ds(pl.multiple_of(zg * GROUP, GROUP), GROUP)
        for i in range(3):
            rs[pl.ds(i, GROUP, stride=8), :] = wd[i, own, :]
        rs[pl.ds(3, GROUP, stride=8), :] = jnp.broadcast_to(lse, (GROUP, DH))
        rs[pl.ds(4, GROUP, stride=8), :] = jnp.broadcast_to(delta, (GROUP, DH))

        @pl.loop(1, GROUP)
        def _(d):
            to_member(d).start()

        pltpu.make_async_copy(rs.at[rows_of(m)], rb.at[rows_of(mine)], p3_recv).start()

    got = pl.ds(0, 8 * HEADS)
    pltpu.make_async_copy(rb.at[got], rb.at[got], p3_recv).wait()

    all_lse = rb[pl.ds(3, 16, stride=8), :]
    all_delta = rb[pl.ds(4, 16, stride=8), :]
    there = lane128 == zg * GROUP + m + 1 - 2 * core

    def at(mask, value):
        return jnp.sum(jnp.where(mask, value, 0.0), 1, keepdims=True)

    lse_r, delta_r = at(here, all_lse), at(here, all_delta)
    lse_f, delta_f = at(there, all_lse), at(there, all_delta)
    p_own = jnp.exp2(ws[0] - lse_r) * weight_wide
    d_own = ((p_own * FACTOR) * (ws[1] - delta_r)).astype(BF16)
    p_cross = jnp.exp2(wx[0] - lse_r)
    d_cross = ((p_cross * FACTOR) * (wx[1] - delta_r)).astype(BF16)
    p_far = jnp.exp2(w2[0] - lse_f)
    d_far = ((p_far * FACTOR) * (w2[1] - delta_f)).astype(BF16)

    def spread(i):
        row = rb[pl.ds(i, 16, stride=8), :]
        return jnp.where(block, jnp.concatenate([row] * HEADS, axis=1), 0.0)

    dq_row = jnp.where(block, mm(d_own, x[1], NN) + mm(d_cross, pr[1], NN), 0.0) + spread(0)
    sel = sel_wide
    fixes = (
        (oq, 0, jnp.concatenate([sel, sel], 0), jnp.concatenate(split(dq_row), 0)),
        (ok, 1, jnp.concatenate([d_own, d_far, sel, sel], 0), jnp.concatenate([qr[0], qp[0], *split(spread(1))], 0)),
        (
            ov,
            2,
            jnp.concatenate([p_own.astype(BF16), p_far.astype(BF16), sel, sel], 0),
            jnp.concatenate([qr[3], qp[1], *split(spread(2))], 0),
        ),
    )
    stores = []
    for ref, i, left, right in fixes:
        ref[...] = (acc[i] + mm(left, right, TN)).astype(BF16)
    for copy in pair_copies:
        copy.wait_send()
    stat_copy.wait_send()
    wait_sent(sb, pb, p1_send, p1_recv)
    wait_sent(sc, pc, c1_send, c1_recv)

    @pl.when(owner)
    def _():
        @pl.loop(1, ZGROUPS)
        def _(d):
            to_zpeer(tt, p2_send, p2_recv, d).wait_send()
            to_zpeer(ts, c2_send, c2_recv, d).wait_send()

        @pl.loop(1, GROUP)
        def _(d):
            to_member(d).wait_send()


def on_device(query, key, value, grad_out, offsets):
    shape = jax.ShapeDtypeStruct((TOK, WIDTH), BF16)
    vmem = pltpu.VMEM
    dma = pltpu.SemaphoreType.DMA
    return pl.pallas_call(
        kernel,
        out_shape=(shape, shape, shape),
        in_specs=[pl.BlockSpec(memory_space=pltpu.MemorySpace.HBM)] * 5,
        out_specs=(pl.BlockSpec(memory_space=vmem),) * 3,
        scratch_shapes=[
            vmem((4, TOK, WIDTH), BF16),
            vmem((4, HALF, WIDTH), BF16),
            vmem((4, HALF, WIDTH), BF16),
            vmem((4, 16, WIDTH), BF16),
            vmem((8 * HEADS, DH), F32),
            vmem((8 * GROUP, DH), F32),
            vmem((8 * HEADS, DH), F32),
            vmem((8 * GROUP, DH), F32),
            vmem((ZGROUPS, 4, GROUP, DH), BF16),
            vmem((ZGROUPS, 2, DH), F32),
            vmem((8 * GROUP, DH), F32),
            vmem((8 * 16, DH), F32),
            vmem((2, 16, HALF), F32),
            vmem((2, 16, HALF), F32),
            vmem((3, TOK, WIDTH), F32),
            vmem((2, 16, TOK), F32),
            vmem((2, 16, TOK), F32),
            vmem((2, 16, HALF), F32),
            vmem((2, 16, TOK), F32),
            vmem((2, 16, WIDTH), BF16),
            vmem((3, 128, DH), F32),
            pltpu.SMEM((2, HEADS), jnp.int32),
            dma((4,)),
            dma(()),
            pltpu.SemaphoreType.REGULAR((6,)),
            dma((4,)),
            dma((4,)),
            dma((HEADS,)),
            dma(()),
            dma((HEADS,)),
            dma(()),
            dma((ZGROUPS,)),
            dma(()),
            dma((ZGROUPS,)),
            dma(()),
            dma((GROUP,)),
            dma(()),
            dma(()),
            dma(()),
        ],
        compiler_params=pltpu.CompilerParams(collective_id=0, has_side_effects=True, vmem_limit_bytes=48 * 1024 * 1024),
    )(*[pltpu.with_memory_space_constraint(a, pltpu.MemorySpace.HBM) for a in (offsets, query, key, value, grad_out)])


def solution(mesh):
    placed = (P("ctx", None),) * 4 + (P(),)
    return jax.shard_map(
        on_device, mesh=mesh, in_specs=placed, out_specs=(P("ctx", None),) * 3, check_vma=False
    )
```

time: 50.2 us -> 39.8 us (0.79)
  Pallas kernels: 41.7 us -> 36.5 us
  local copies, waits for them, and re-layouts: 7.53 us -> 2.51 us
    pallas_call x1, Pallas kernels: 41.7 us -> 36.5 us  [on_device(): pl.pallas_call(kernel, out_shape=(shape, shape, shape), in_specs=[pl.Bloc...]
    unnamed x13 -> x3, local copies, waits for them, and re-layouts: 7.53 us -> 2.51 us
where the time goes in v2:
time: 39.8 us; the launch traced here: 39.6 us
  Pallas kernels  36.5 us (92%)
  local copies, waits for them, and re-layouts  2.51 us (6%)
  between operations  0.64 us (2%)
    pallas_call x1, Pallas kernels, on_device(): pl.pallas_call(kernel, out_shape=(shape, shape, shape), in_specs=[pl.Bloc...  36.5 us
    unnamed x3, local copies, waits for them, and re-layouts  2.51 us

profile of v2, /device:TPU:1, one launch (start us, length us, event | category | flops | bytes accessed | tf_op | source)
XLA Modules:
  0.0 39.6 jit_solution(18425394301810105999)
XLA Ops:
  0.6 36.5 %shard_map.76 = (bf16[256,1280]{1,0:T(8,128)(2,1)S(1)}, bf16[256,1280]{1,0:T(8,128)(2,1)S(1)}, bf16[256,1280]{1,0:T(8,128)(2,1)S(1)}) custom-call(s32[2,10]{1,0:T(2,128)} %off_hbm.1, bf16[256,1280]{1,0:T(8,128)(2,1)} %q_hbm.1, bf16[256,1280]{1,0:T(8,128)(2,1)} %k_hbm.1, bf16[256,1280]{1,0:T(8,128)(2,1)} %v_hbm.1, bf16[256,1280]{1,0:T(8,128)(2,1)} %g_hbm.1), custom_call_target="tpu_custom_call" | custom-call | tf_op jit(solution)/shard_map/pallas_call | solution.py:441
  37.1 0.8 %copy.11 = bf16[256,1280]{1,0:T(8,128)(2,1)} copy(bf16[256,1280]{1,0:T(8,128)(2,1)S(1)} %get-tuple-element.6) | data formatting | bytes 1310720
  37.9 0.8 %copy.12 = bf16[256,1280]{1,0:T(8,128)(2,1)} copy(bf16[256,1280]{1,0:T(8,128)(2,1)S(1)} %get-tuple-element.7) | data formatting | bytes 1310720
  38.8 0.8 %copy.13 = bf16[256,1280]{1,0:T(8,128)(2,1)} copy(bf16[256,1280]{1,0:T(8,128)(2,1)S(1)} %get-tuple-element.8) | data formatting | bytes 1310720

commit v3 on v2

--- a/solution.py
+++ b/solution.py
@@ -16,9 +16,9 @@
 FACTOR = DH**-0.5
 SCALE2 = FACTOR * 1.4426950408889634
 LOW = -1e30
-UNROLL = 2
+PAIRS = HEADS // 2
+CROSS_FIRST = 3
 EARLY = 1
-MIDDLE = 2
 F32 = jnp.float32
 BF16 = jnp.bfloat16
 
@@ -41,8 +41,8 @@
 
 
 def kernel(
-    off_hbm, q_hbm, k_hbm, v_hbm, g_hbm, oq, ok, ov,
-    x, px, pr, qr, sb, pb, sc, pc, tt, ts, rs, rb, lx, lr, acc, ls, ws, wx, w2, qp, wd, off,
+    off_hbm, q_hbm, k_hbm, v_hbm, g_hbm, acc, left, fix,
+    x, px, pr, qr, sb, pb, sc, pc, tt, ts, rs, rb, lx, lr, ls, ws, wx, w2, qp, wd, off,
     ld_sem, off_sem, ready, px_send, px_recv, p1_send, p1_recv, c1_send, c1_recv,
     p2_send, p2_recv, c2_send, c2_recv, p3_send, p3_recv, lx_send, lx_recv,
 ):
@@ -75,16 +75,6 @@
             src_ref=src, dst_ref=dst, send_sem=send, recv_sem=recv, device_id=device, device_id_type=MESH
         )
 
-    barrier = pltpu.get_barrier_semaphore()
-    right = zpeer(lax.rem(zg + 1, ZGROUPS))
-    left = zpeer(lax.rem(zg + ZGROUPS - 1, ZGROUPS))
-    pl.semaphore_signal(barrier, inc=1, device_id=right, device_id_type=MESH)
-    pl.semaphore_signal(barrier, inc=1, device_id=left, device_id_type=MESH)
-
-    @pl.loop(1, GROUP)
-    def _(d):
-        pl.semaphore_signal(barrier, inc=1, device_id=member(lax.rem(m + d, GROUP)), device_id_type=MESH)
-
     off_load = pltpu.make_async_copy(off_hbm, off, off_sem)
     off_load.start()
     loads = [
@@ -93,6 +83,16 @@
     for i in (1, 2, 0, 3):
         loads[i].start()
 
+    barrier = pltpu.get_barrier_semaphore()
+    upper = zpeer(lax.rem(zg + 1, ZGROUPS))
+    lower = zpeer(lax.rem(zg + ZGROUPS - 1, ZGROUPS))
+    pl.semaphore_signal(barrier, inc=1, device_id=upper, device_id_type=MESH)
+    pl.semaphore_signal(barrier, inc=1, device_id=lower, device_id_type=MESH)
+
+    @pl.loop(1, GROUP)
+    def _(d):
+        pl.semaphore_signal(barrier, inc=1, device_id=member(lax.rem(m + d, GROUP)), device_id_type=MESH)
+
     def pass_on(stage):
         @pl.when(owner)
         def _():
@@ -100,8 +100,8 @@
                 pl.semaphore_wait(ready.at[2 * stage - 2], 1)
                 pl.semaphore_wait(ready.at[2 * stage - 1], 1)
             if stage < 3:
-                pl.semaphore_signal(ready.at[2 * stage], inc=1, device_id=right, device_id_type=MESH)
-                pl.semaphore_signal(ready.at[2 * stage + 1], inc=1, device_id=left, device_id_type=MESH)
+                pl.semaphore_signal(ready.at[2 * stage], inc=1, device_id=upper, device_id_type=MESH)
+                pl.semaphore_signal(ready.at[2 * stage + 1], inc=1, device_id=lower, device_id_type=MESH)
 
     sb[...] = jnp.zeros_like(sb)
     sc[...] = jnp.zeros_like(sc)
@@ -163,12 +163,11 @@
 
     loads[1].wait()
     pack_pair(1)
-    loads[2].wait()
-    pack_pair(2)
-
     pl.semaphore_wait(barrier, GROUP + 1)
     pass_on(0)
     pair_copies[1].start()
+    loads[2].wait()
+    pack_pair(2)
     pair_copies[2].start()
 
     loads[0].wait()
@@ -184,6 +183,7 @@
     x_own = mm(qr[3], x[2], NT)
     pair_copies[1].wait_recv()
     pair_copies[2].wait_recv()
+    pass_on(1)
     s_cross = jnp.where(row_in_pair[:, :HALF], mm(qr[0], pr[1], NT) * SCALE2, LOW)
     x_cross = mm(qr[3], pr[2], NT)
     peak = jnp.maximum(jnp.max(s_own, 1, keepdims=True), jnp.max(s_cross, 1, keepdims=True))
@@ -203,7 +203,6 @@
     ws[1] = x_own
     wx[0] = s_cross
     wx[1] = x_cross
-    pass_on(1)
     pack_pair(0)
     pair_copies[0].start()
     pack_pair(3)
@@ -221,8 +220,18 @@
     def peak_of(a):
         return jnp.max(jnp.max(a, 0), 0, keepdims=True)
 
+    def lanes(h):
+        return pl.ds(pl.multiple_of(h * DH, DH), DH)
+
+    def two_lanes(j):
+        return pl.ds(pl.multiple_of(j * 2 * DH, 2 * DH), 2 * DH)
+
+    def diagonal(a, b):
+        blank = jnp.zeros_like(a)
+        return jnp.concatenate([jnp.concatenate([a, blank], 1), jnp.concatenate([blank, b], 1)], 0)
+
     def attend(h):
-        hs = pl.ds(pl.multiple_of(h * DH, DH), DH)
+        hs = lanes(h)
         qh = x[0, :, hs]
         gh = x[3, :, hs]
         kh = x[1, :, hs]
@@ -252,47 +261,43 @@
         d1 = ((e1 * slope) * (x1 - delta)).reshape(HALF, TOK).astype(BF16)
         acc[2, :, hs] = mm(p0.reshape(TOK, TOK).astype(BF16), gh, NN)
         acc[1, :, hs] = mm(d0, qh, NN)
-        acc[0, :, hs] = mm(d0, kh, TN) + mm(d1, kx, TN)
-
-    @pl.loop(0, EARLY)
-    def _(j):
-        for u in range(UNROLL):
-            attend(j * UNROLL + u)
+        return mm(d0, kh, TN), d1, kx
+
+    def attend_two(j):
+        own_a, far_a, kx_a = attend(2 * j)
+        own_b, far_b, kx_b = attend(2 * j + 1)
+        far = mm(jnp.concatenate([far_a, far_b], 0), diagonal(kx_a, kx_b), TN)
+        acc[0, :, two_lanes(j)] = jnp.concatenate([own_a, own_b], 1) + far
 
     def to_zpeer(src, send, recv, d):
         return remote(src.at[zg], src.at[zg], send.at[d], recv, zpeer(lax.rem(zg + d, ZGROUPS)))
-
-    pass_on(3)
 
     @pl.when(owner)
     def _():
         pltpu.make_async_copy(pb, pb, p1_recv).wait()
         for i in range(4):
             tt[zg, i] = pb[pl.ds(i, GROUP, stride=8), :].astype(BF16)
-
-        @pl.loop(1, ZGROUPS)
-        def _(d):
+        for d in (3, 5, 2, 6, 1, 7):
             to_zpeer(tt, p2_send, p2_recv, d).start()
 
-    @pl.loop(EARLY, MIDDLE)
+    @pl.loop(0, EARLY)
     def _(j):
-        for u in range(UNROLL):
-            attend(j * UNROLL + u)
+        attend_two(j)
+
+    pass_on(3)
 
     @pl.when(owner)
     def _():
+        to_zpeer(tt, p2_send, p2_recv, 4).start()
         pltpu.make_async_copy(pc, pc, c1_recv).wait()
         for i in range(2):
             ts[zg, i : i + 1, :] = jnp.sum(pc[pl.ds(i, GROUP, stride=8), :], 0, keepdims=True)
-
-        @pl.loop(1, ZGROUPS)
-        def _(d):
+        for d in (4, 3, 5, 2, 6, 1, 7):
             to_zpeer(ts, c2_send, c2_recv, d).start()
 
-    @pl.loop(MIDDLE, HEADS // UNROLL)
+    @pl.loop(EARLY, PAIRS)
     def _(j):
-        for u in range(UNROLL):
-            attend(j * UNROLL + u)
+        attend_two(j)
 
     perm_t = jnp.where(iota((TOK, TOK), 1) < HALF, 2 * iota((TOK, TOK), 1), 2 * iota((TOK, TOK), 1) - (TOK - 1))
     perm_t = (iota((TOK, TOK), 0) == perm_t).astype(F32).astype(BF16)
@@ -307,35 +312,31 @@
 
     pair_copies[0].wait_recv()
     pair_copies[3].wait_recv()
-    lane_pair = iota((16, HALF), 1)
-    sel_pair = jnp.logical_and(row_in_pair[:, :HALF], lane_pair == lax.div(off1[:, :HALF], 2))
-    sel_pair = sel_pair.astype(F32).astype(BF16)
-    qp[0] = jnp.where(block, mm(sel_pair, pr[0], NN), 0.0).astype(BF16)
-    qp[1] = jnp.where(block, mm(sel_pair, pr[3], NN), 0.0).astype(BF16)
-    w2[0] = jnp.where(both, mm(qp[0], x[1], NT) * SCALE2, LOW)
-    w2[1] = mm(qp[1], x[2], NT)
-
     stat_copy.wait_recv()
 
     def cross(h):
-        hs = pl.ds(pl.multiple_of(h * DH, DH), DH)
-        kh = x[1, :, hs]
-        vh = x[2, :, hs]
+        hs = lanes(h)
         qx = pr[0, :, hs]
         gx = pr[3, :, hs]
         lse = lr[0, pl.ds(h, 1), :]
         delta = lr[1, pl.ds(h, 1), :]
-        s2 = (mm(kh, qx, NT) * SCALE2).reshape(TOK // 8, 8, HALF)
-        x2 = mm(vh, gx, NT).reshape(TOK // 8, 8, HALF)
+        both_in = mm(jnp.concatenate([x[1, :, hs], x[2, :, hs]], 1), diagonal(qx, gx), NT)
+        s2 = (both_in[:, :HALF] * SCALE2).reshape(TOK // 8, 8, HALF)
+        x2 = both_in[:, HALF:].reshape(TOK // 8, 8, HALF)
         p2 = jnp.exp2(jnp.where(parity_sub[:, :, :HALF] == off[0, h], s2 - lse, LOW))
         d2 = ((p2 * FACTOR) * (x2 - delta)).reshape(TOK, HALF).astype(BF16)
-        acc[2, :, hs] += mm(p2.reshape(TOK, HALF).astype(BF16), gx, NN)
-        acc[1, :, hs] += mm(d2, qx, NN)
-
-    @pl.loop(0, HEADS // UNROLL)
+        p2 = p2.reshape(TOK, HALF).astype(BF16)
+        both_out = mm(jnp.concatenate([p2, d2], 1), diagonal(gx, qx), NN)
+        acc[2, :, hs] += both_out[:, :DH]
+        acc[1, :, hs] += both_out[:, DH:]
+
+    def cross_two(j):
+        cross(2 * j)
+        cross(2 * j + 1)
+
+    @pl.loop(0, CROSS_FIRST)
     def _(j):
-        for u in range(UNROLL):
-            cross(j * UNROLL + u)
+        cross_two(j)
 
     def to_member(d):
         j = lax.rem(m + d, GROUP)
@@ -378,6 +379,35 @@
 
         pltpu.make_async_copy(rs.at[rows_of(m)], rb.at[rows_of(mine)], p3_recv).start()
 
+    @pl.loop(CROSS_FIRST, PAIRS)
+    def _(j):
+        cross_two(j)
+
+    lane_pair = iota((16, HALF), 1)
+    sel_pair = jnp.logical_and(row_in_pair[:, :HALF], lane_pair == lax.div(off1[:, :HALF], 2))
+    sel_pair = sel_pair.astype(F32).astype(BF16)
+    qp[0] = jnp.where(block, mm(sel_pair, pr[0], NN), 0.0).astype(BF16)
+    qp[1] = jnp.where(block, mm(sel_pair, pr[3], NN), 0.0).astype(BF16)
+    w2[0] = jnp.where(both, mm(qp[0], x[1], NT) * SCALE2, LOW)
+    w2[1] = mm(qp[1], x[2], NT)
+
+    for copy in pair_copies:
+        copy.wait_send()
+    stat_copy.wait_send()
+    wait_sent(sb, pb, p1_send, p1_recv)
+    wait_sent(sc, pc, c1_send, c1_recv)
+
+    @pl.when(owner)
+    def _():
+        @pl.loop(1, ZGROUPS)
+        def _(d):
+            to_zpeer(tt, p2_send, p2_recv, d).wait_send()
+            to_zpeer(ts, c2_send, c2_recv, d).wait_send()
+
+        @pl.loop(1, GROUP)
+        def _(d):
+            to_member(d).wait_send()
+
     got = pl.ds(0, 8 * HEADS)
     pltpu.make_async_copy(rb.at[got], rb.at[got], p3_recv).wait()
 
@@ -403,44 +433,37 @@
 
     dq_row = jnp.where(block, mm(d_own, x[1], NN) + mm(d_cross, pr[1], NN), 0.0) + spread(0)
     sel = sel_wide
-    fixes = (
-        (oq, 0, jnp.concatenate([sel, sel], 0), jnp.concatenate(split(dq_row), 0)),
-        (ok, 1, jnp.concatenate([d_own, d_far, sel, sel], 0), jnp.concatenate([qr[0], qp[0], *split(spread(1))], 0)),
-        (
-            ov,
-            2,
-            jnp.concatenate([p_own.astype(BF16), p_far.astype(BF16), sel, sel], 0),
-            jnp.concatenate([qr[3], qp[1], *split(spread(2))], 0),
-        ),
-    )
+    blank_left = jnp.zeros((32, TOK), BF16)
+    blank_right = jnp.zeros((32, WIDTH), BF16)
+    left[0] = jnp.concatenate([sel, sel, blank_left], 0)
+    fix[0] = jnp.concatenate([*split(dq_row), blank_right], 0)
+    left[1] = jnp.concatenate([d_own, d_far, sel, sel], 0)
+    fix[1] = jnp.concatenate([qr[0], qp[0], *split(spread(1))], 0)
+    left[2] = jnp.concatenate([p_own.astype(BF16), p_far.astype(BF16), sel, sel], 0)
+    fix[2] = jnp.concatenate([qr[3], qp[1], *split(spread(2))], 0)
+
+
+def finish(acc, left, fix, oq, ok, ov, held, sem):
     stores = []
-    for ref, i, left, right in fixes:
-        ref[...] = (acc[i] + mm(left, right, TN)).astype(BF16)
-    for copy in pair_copies:
-        copy.wait_send()
-    stat_copy.wait_send()
-    wait_sent(sb, pb, p1_send, p1_recv)
-    wait_sent(sc, pc, c1_send, c1_recv)
-
-    @pl.when(owner)
-    def _():
-        @pl.loop(1, ZGROUPS)
-        def _(d):
-            to_zpeer(tt, p2_send, p2_recv, d).wait_send()
-            to_zpeer(ts, c2_send, c2_recv, d).wait_send()
-
-        @pl.loop(1, GROUP)
-        def _(d):
-            to_member(d).wait_send()
+    for i, ref in enumerate((oq, ok, ov)):
+        held[i] = (acc[i] + mm(left[i], fix[i], TN)).astype(BF16)
+        stores.append(pltpu.make_async_copy(held.at[i], ref, sem.at[i]))
+        stores[i].start()
+    for store in stores:
+        store.wait()
 
 
 def on_device(query, key, value, grad_out, offsets):
     shape = jax.ShapeDtypeStruct((TOK, WIDTH), BF16)
     vmem = pltpu.VMEM
     dma = pltpu.SemaphoreType.DMA
-    return pl.pallas_call(
+    acc, left, fix = pl.pallas_call(
         kernel,
-        out_shape=(shape, shape, shape),
+        out_shape=(
+            jax.ShapeDtypeStruct((3, TOK, WIDTH), F32),
+            jax.ShapeDtypeStruct((3, 64, TOK), BF16),
+            jax.ShapeDtypeStruct((3, 64, WIDTH), BF16),
+        ),
         in_specs=[pl.BlockSpec(memory_space=pltpu.MemorySpace.HBM)] * 5,
         out_specs=(pl.BlockSpec(memory_space=vmem),) * 3,
         scratch_shapes=[
@@ -458,7 +481,6 @@
             vmem((8 * 16, DH), F32),
             vmem((2, 16, HALF), F32),
             vmem((2, 16, HALF), F32),
-            vmem((3, TOK, WIDTH), F32),
             vmem((2, 16, TOK), F32),
             vmem((2, 16, TOK), F32),
             vmem((2, 16, HALF), F32),
@@ -486,6 +508,14 @@
         ],
         compiler_params=pltpu.CompilerParams(collective_id=0, has_side_effects=True, vmem_limit_bytes=48 * 1024 * 1024),
     )(*[pltpu.with_memory_space_constraint(a, pltpu.MemorySpace.HBM) for a in (offsets, query, key, value, grad_out)])
+    return pl.pallas_call(
+        finish,
+        out_shape=(shape, shape, shape),
+        in_specs=[pl.BlockSpec(memory_space=vmem)] * 3,
+        out_specs=(pl.BlockSpec(memory_space=pl.ANY),) * 3,
+        scratch_shapes=[vmem((3, TOK, WIDTH), BF16), dma((3,))],
+        compiler_params=pltpu.CompilerParams(vmem_limit_bytes=8 * 1024 * 1024),
+    )(acc, left, fix)
 
 
 def solution(mesh):

time: 39.8 us -> 35.8 us (0.90)
  local copies, waits for them, and re-layouts: 2.51 us -> 0 us
  Pallas kernels: 36.5 us -> 35 us
    unnamed x3 -> x0, local copies, waits for them, and re-layouts: 2.51 us -> none
    pallas_call x1 -> x2, Pallas kernels: 36.5 us -> 35 us  [the longest x1 33.4 us: on_device(): pl.pallas_call(kernel, out_shape=(jax.ShapeDtypeStruct((3, TOK, WIDTH), F...]
where the time goes in v3:
time: 35.8 us; the launch traced here: 35.7 us
  Pallas kernels  35 us (98%)
  between operations  0.64 us (2%)
    pallas_call x1, Pallas kernels, on_device(): pl.pallas_call(kernel, out_shape=(jax.ShapeDtypeStruct((3, TOK, WIDTH), F...  33.4 us
    pallas_call x1, Pallas kernels, on_device(): pl.pallas_call(finish, out_shape=(shape, shape, shape), in_specs=[pl.Bloc...  1.65 us

profile of v3, /device:TPU:1, one launch (start us, length us, event | category | flops | bytes accessed | tf_op | source)
XLA Modules:
  0.0 35.7 jit_solution(9530158878573141491)
XLA Ops:
  0.6 33.4 %shard_map.76 = (f32[3,256,1280]{2,1,0:T(8,128)S(1)}, bf16[3,64,256]{2,1,0:T(8,128)(2,1)S(1)}, bf16[3,64,1280]{2,1,0:T(8,128)(2,1)S(1)}) custom-call(s32[2,10]{1,0:T(2,128)} %off_hbm.1, bf16[256,1280]{1,0:T(8,128)(2,1)} %q_hbm.1, bf16[256,1280]{1,0:T(8,128)(2,1)} %k_hbm.1, bf16[256,1280]{1,0:T(8,128)(2,1)} %v_hbm.1, bf16[256,1280]{1,0:T(8,128)(2,1)} %g_hbm.1), custom_call_target="tpu_custom_call" | custom-call | tf_op jit(solution)/shard_map/pallas_call | solution.py:460
  34.0 1.6 %shard_map.77 = (bf16[256,1280]{1,0:T(8,128)(2,1)}, bf16[256,1280]{1,0:T(8,128)(2,1)}, bf16[256,1280]{1,0:T(8,128)(2,1)}) custom-call(f32[3,256,1280]{2,1,0:T(8,128)S(1)} %get-tuple-element.6.acc, bf16[3,64,256]{2,1,0:T(8,128)(2,1)S(1)} %get-tuple-element.7.left, bf16[3,64,1280]{2,1,0:T(8,128)(2,1)S(1)} %get-tuple-element.8.fix), custom_call_target="tpu_custom_call" | custom-call | tf_op jit(solution)/shard_map/pallas_call | solution.py:511

commit v4 on v3

v4 whole, which is shorter than its diff:
```python
import jax
import jax.numpy as jnp
from jax import lax
from jax.experimental import pallas as pl
from jax.experimental.pallas import tpu as pltpu
from jax.sharding import PartitionSpec as P

MESH = pl.DeviceIdType.MESH
HEADS = 10
DH = 128
TOK = 256
HALF = TOK // 2
WIDTH = HEADS * DH
GROUP = 16
ZGROUPS = 8
FACTOR = DH**-0.5
SCALE2 = FACTOR * 1.4426950408889634
LOW = -1e30
PAIRS = HEADS // 2
CROSS_FIRST = 3
F32 = jnp.float32
BF16 = jnp.bfloat16

NN = (((1,), (0,)), ((), ()))
NT = (((1,), (1,)), ((), ()))
TN = (((0,), (0,)), ((), ()))


def mm(a, b, dims):
    return lax.dot_general(a, b, dims, preferred_element_type=F32)


def iota(shape, dim):
    return lax.broadcasted_iota(jnp.int32, shape, dim)


def split(x):
    high = x.astype(BF16)
    return high, (x - high.astype(F32)).astype(BF16)


def kernel(
    off_hbm, q_hbm, k_hbm, v_hbm, g_hbm, acc, left, fix,
    x, px, pr, qr, sb, pb, sc, pc, tt, ts, rs, rb, lx, lr, ls, ws, wx, w2, qp, wd, off, sa, sb2, ta, tb, da, db, ua, ub, ea, eb,
    ld_sem, off_sem, ready, px_send, px_recv, p1_send, p1_recv, c1_send, c1_recv,
    p2_send, p2_recv, c2_send, c2_recv, p3_send, p3_recv, lx_send, lx_recv, qp_send, qp_recv,
):
    me = lax.axis_index("ctx")
    core = lax.rem(me, 2)
    z = lax.rem(lax.div(me, 2), 16)
    y = lax.rem(lax.div(me, 32), 4)
    base = lax.div(me, 128) * 128
    zg = lax.div(z, 2)
    zl = lax.rem(z, 2)
    m = y * 4 + zl * 2 + core
    turned = lax.rem(zl + lax.div(zg, 4), 2)
    drift = core * (1 - turned)
    mine = (core * 2 + turned) * 4 + lax.rem(y + 2 * lax.rem(zg, 2) * drift, 4)
    owner = mine < HEADS

    def member(j):
        return (base + lax.div(j, 4) * 32 + (zg * 2 + lax.rem(lax.div(j, 2), 2)) * 2 + lax.rem(j, 2),)

    def zpeer(d):
        g = lax.rem(zg + d, ZGROUPS)
        row = lax.rem(y + 2 * (d % 2) * drift, 4)
        return (base + row * 32 + (g * 2 + lax.rem(turned + lax.div(g, 4), 2)) * 2 + core,)

    def owner_of(h):
        k = lax.div(h, 4)
        row = lax.rem(lax.rem(h, 4) + 2 * lax.rem(zg, 2) * lax.div(k, 2), 4)
        return row * 4 + lax.rem(lax.rem(k, 2) + lax.div(zg, 4), 2) * 2 + lax.div(k, 2)

    partner = (me + 1 - 2 * core,)

    def remote(src, dst, send, recv, device):
        return pltpu.make_async_remote_copy(
            src_ref=src, dst_ref=dst, send_sem=send, recv_sem=recv, device_id=device, device_id_type=MESH
        )

    off_load = pltpu.make_async_copy(off_hbm, off, off_sem)
    off_load.start()
    loads = [
        pltpu.make_async_copy(ref, x.at[i], ld_sem.at[i]) for i, ref in enumerate((q_hbm, k_hbm, v_hbm, g_hbm))
    ]
    for i in (1, 2, 0, 3):
        loads[i].start()

    barrier = pltpu.get_barrier_semaphore()
    upper = zpeer(1)
    lower = zpeer(ZGROUPS - 1)
    upper2 = zpeer(2)
    lower2 = zpeer(ZGROUPS - 2)
    for there in (upper2, lower2, upper, lower):
        pl.semaphore_signal(barrier, inc=1, device_id=there, device_id_type=MESH)

    plane = base + zg * 4
    ys = [lax.rem(y + i, 4) * 32 for i in range(4)]
    zs = [zl * 2, 2 - zl * 2]
    cs = [core, 1 - core]
    for i in range(1, GROUP):
        there = plane + ys[i // 4] + (zs[i // 2 % 2] + cs[i % 2])
        pl.semaphore_signal(barrier, inc=1, device_id=(there,), device_id_type=MESH)

    def near_groups_ready():
        @pl.when(owner)
        def _():
            pl.semaphore_signal(ready.at[0], inc=1, device_id=upper2, device_id_type=MESH)
            pl.semaphore_signal(ready.at[1], inc=1, device_id=lower2, device_id_type=MESH)

    def far_groups_ready():
        @pl.when(owner)
        def _():
            pl.semaphore_wait(ready.at[0], 1)
            pl.semaphore_wait(ready.at[1], 1)

    sb[...] = jnp.zeros_like(sb)
    sc[...] = jnp.zeros_like(sc)
    rb[...] = jnp.zeros_like(rb)
    rs[...] = jnp.zeros_like(rs)
    ls[...] = jnp.zeros_like(ls)
    perm_row = iota((TOK, TOK), 0)
    perm_to = jnp.where(perm_row < HALF, 2 * perm_row, 2 * perm_row - (TOK - 1))
    perm = (iota((TOK, TOK), 1) == perm_to).astype(F32).astype(BF16)
    block = lax.div(iota((16, WIDTH), 1), DH) == iota((16, WIDTH), 0)
    lane_head = lax.div(iota((8, WIDTH), 1), DH)
    row16 = iota((16, TOK), 0)
    lane16 = iota((16, TOK), 1)

    off_load.wait()
    off_lane = jnp.zeros((8, WIDTH), jnp.int32)
    off0 = jnp.zeros((16, TOK), jnp.int32)
    off1 = jnp.zeros((16, TOK), jnp.int32)
    for h in range(HEADS):
        off_lane = jnp.where(lane_head == h, off[0, h], off_lane)
        off0 = jnp.where(row16 == h, off[0, h], off0)
        off1 = jnp.where(row16 == h, off[1, h], off1)
    sel_wide = (lane16 == off1).astype(F32).astype(BF16)
    row_in_pair = lax.rem(off1, 2) == off0
    key_in_pair = lax.rem(lane16, 2) == off0
    both = jnp.logical_and(row_in_pair, key_in_pair)
    weight_wide = jnp.where(both, 2.0, 1.0)
    off_wide = off_lane[0:1, :] > 0

    def pack_pair(i):
        parts = mm(perm, x[i], NN)
        px[i] = jnp.where(off_wide, parts[HALF:], parts[:HALF]).astype(BF16)

    pair_copies = [remote(px.at[i], pr.at[i], px_send.at[i], px_recv.at[i], partner) for i in range(4)]

    def rows_of(j):
        return pl.ds(pl.multiple_of(8 * j, 8), 8)

    def to_owner(src, dst, send, recv, h):
        return remote(src.at[rows_of(h)], dst.at[rows_of(m)], send.at[h], recv, member(owner_of(h)))

    def send_to_owners(src, dst, send, recv):
        @pl.loop(0, HEADS)
        def _(h):
            @pl.when(owner_of(h) != m)
            def _():
                to_owner(src, dst, send, recv, h).start()

            @pl.when(owner_of(h) == m)
            def _():
                pltpu.make_async_copy(src.at[rows_of(h)], dst.at[rows_of(m)], recv).start()

    def wait_sent(src, dst, send, recv):
        @pl.loop(0, HEADS)
        def _(h):
            @pl.when(owner_of(h) != m)
            def _():
                to_owner(src, dst, send, recv, h).wait_send()

    loads[1].wait()
    pack_pair(1)
    loads[2].wait()
    pack_pair(2)
    loads[0].wait()
    loads[3].wait()
    for i in range(4):
        picked = jnp.where(block, mm(sel_wide, x[i], NN), 0.0)
        qr[i] = picked.astype(BF16)
        for h in range(HEADS):
            sb[8 * h + i : 8 * h + i + 1, :] = picked[h : h + 1, h * DH : (h + 1) * DH]

    s_own = mm(qr[0], x[1], NT) * SCALE2
    x_own = mm(qr[3], x[2], NT)
    ws[0] = s_own
    ws[1] = x_own
    lane128 = iota((16, DH), 1)
    token = zg * GROUP + m
    here = lane128 == token
    other = lane128 == token + 1 - 2 * core

    def statistics(s, value, weight, row, at):
        peak = jnp.max(s, 1, keepdims=True)
        e = jnp.exp2(s - peak)
        e = e if weight is None else e * weight
        total = jnp.sum(e, 1, keepdims=True)
        blend = jnp.sum(e * value, 1, keepdims=True)
        lse = jnp.where(at, peak + jnp.log2(total), 0.0)
        delta = jnp.where(at, blend / total, 0.0)
        for h in range(HEADS):
            sc[8 * h + row : 8 * h + row + 1, :] = lse[h : h + 1, :]
            sc[8 * h + row + 1 : 8 * h + row + 2, :] = delta[h : h + 1, :]

    statistics(s_own, x_own, weight_wide, 0, here)

    pl.semaphore_wait(barrier, GROUP + 3)
    near_groups_ready()
    wide_copies = [remote(qr.at[3 * i], qp.at[i], qp_send.at[i], qp_recv.at[i], partner) for i in range(2)]
    for copy in wide_copies:
        copy.start()
    send_to_owners(sb, pb, p1_send, p1_recv)
    pair_copies[1].start()
    pair_copies[2].start()

    for copy in wide_copies:
        copy.wait_recv()
    s_far = jnp.where(both, mm(qp[0], x[1], NT) * SCALE2, LOW)
    x_far = mm(qp[1], x[2], NT)
    statistics(s_far, x_far, None, 2, other)
    send_to_owners(sc, pc, c1_send, c1_recv)
    w2[0] = s_far
    w2[1] = x_far

    pack_pair(0)
    pair_copies[0].start()
    pack_pair(3)
    pair_copies[3].start()

    lane_row = iota((1, TOK), 1)
    parity_lane = lax.rem(lane_row, 2)
    parity_sub = lax.rem(iota((1, 8, TOK), 1), 2)
    parity_both = lax.rem(iota((1, 8, TOK), 2), 2)

    def total_of(a):
        return jnp.sum(jnp.sum(a, 0), 0, keepdims=True)

    def peak_of(a):
        return jnp.max(jnp.max(a, 0), 0, keepdims=True)

    def lanes(h):
        return pl.ds(pl.multiple_of(h * DH, DH), DH)

    def products(h, sx, top_ref):
        hs = lanes(h)
        qh = x[0, :, hs]
        gh = x[3, :, hs]
        s0 = mm(x[1, :, hs], qh, NT) * SCALE2
        s1 = mm(pr[1, :, hs], qh, NT) * SCALE2 + jnp.where(parity_lane == off[0, h], 0.0, LOW)
        sx[0, :TOK, :] = s0
        sx[0, TOK:, :] = s1
        sx[1, :TOK, :] = mm(x[2, :, hs], gh, NT)
        sx[1, TOK:, :] = mm(pr[2, :, hs], gh, NT)
        top = jnp.maximum(peak_of(s0.reshape(TOK // 8, 8, TOK)), peak_of(s1.reshape(HALF // 8, 8, TOK)))
        top_ref[...] = top

    def weigh(h, sx, top_ref, pd):
        top = top_ref[...]
        keep = jnp.where(lane_row == off[1, h], 0.0, 1.0)
        twice = jnp.logical_and(parity_sub == off[0, h], parity_both == off[0, h])
        lifted = top[None] - jnp.where(twice, 1.0, 0.0)
        e0 = jnp.exp2(sx[0, :TOK, :].reshape(TOK // 8, 8, TOK) - lifted)
        e1 = jnp.exp2(sx[0, TOK:, :].reshape(HALF // 8, 8, TOK) - top)
        x0 = sx[1, :TOK, :].reshape(TOK // 8, 8, TOK)
        x1 = sx[1, TOK:, :].reshape(HALF // 8, 8, TOK)
        tot = total_of(e0) + total_of(e1)
        num = total_of(e0 * x0) + total_of(e1 * x1)
        inv = 1.0 / tot
        delta = num * inv
        ls[0, pl.ds(h, 1), :] = jnp.where(keep > 0, top + jnp.log2(tot), -LOW)
        ls[1, pl.ds(h, 1), :] = delta
        gain = inv * keep
        slope = gain * FACTOR
        pd[:TOK, :] = (e0 * gain).reshape(TOK, TOK).astype(BF16)
        pd[TOK : 2 * TOK, :] = ((e0 * slope) * (x0 - delta)).reshape(TOK, TOK).astype(BF16)
        pd[2 * TOK :, :] = ((e1 * slope) * (x1 - delta)).reshape(HALF, TOK).astype(BF16)

    def gather(h, pd):
        hs = lanes(h)
        acc[2, :, hs] = mm(pd[:TOK, :], x[3, :, hs], NN)
        acc[1, :, hs] = mm(pd[TOK : 2 * TOK, :], x[0, :, hs], NN)
        acc[0, :, hs] = mm(pd[TOK : 2 * TOK, :], x[1, :, hs], TN) + mm(pd[2 * TOK :, :], pr[1, :, hs], TN)

    def to_zpeer(src, send, recv, d):
        return remote(src.at[zg], src.at[zg], send.at[d], recv, zpeer(d))

    far_groups_ready()
    @pl.when(owner)
    def _():
        pltpu.make_async_copy(pb, pb, p1_recv).wait()
        for i in range(4):
            tt[zg, i] = pb[pl.ds(i, GROUP, stride=8), :].astype(BF16)
        for d in (4, 3, 5, 2, 6, 1, 7):
            to_zpeer(tt, p2_send, p2_recv, d).start()

    pair_copies[1].wait_recv()
    pair_copies[2].wait_recv()
    products(0, sa, ta)
    weigh(0, sa, ta, da)
    products(1, sb2, tb)
    gather(0, da)
    weigh(1, sb2, tb, db)
    products(2, sa, ta)

    @pl.when(owner)
    def _():
        pltpu.make_async_copy(pc, pc, c1_recv).wait()
        for i in range(4):
            ts[zg, i : i + 1, :] = jnp.sum(pc[pl.ds(i, GROUP, stride=8), :], 0, keepdims=True)
        for d in (4, 3, 5, 2, 6, 1, 7):
            to_zpeer(ts, c2_send, c2_recv, d).start()

    @pl.loop(1, PAIRS)
    def _(j):
        gather(2 * j - 1, db)
        weigh(2 * j, sa, ta, da)
        products(2 * j + 1, sb2, tb)
        gather(2 * j, da)
        weigh(2 * j + 1, sb2, tb, db)
        products(jnp.minimum(2 * j + 2, HEADS - 1), sa, ta)

    gather(HEADS - 1, db)

    perm_t = jnp.where(iota((TOK, TOK), 1) < HALF, 2 * iota((TOK, TOK), 1), 2 * iota((TOK, TOK), 1) - (TOK - 1))
    perm_t = (iota((TOK, TOK), 0) == perm_t).astype(F32).astype(BF16)
    for i in range(2):
        value = ls[i]
        high, rest = split(value)
        mid, least = split(value - high.astype(F32))
        moved = mm(high, perm_t, NN) + (mm(mid, perm_t, NN) + mm(least, perm_t, NN))
        lx[i] = jnp.where(off0[:, :HALF] > 0, moved[:, HALF:], moved[:, :HALF])
    stat_copy = remote(lx, lr, lx_send, lx_recv, partner)
    stat_copy.start()

    pair_copies[0].wait_recv()
    pair_copies[3].wait_recv()
    stat_copy.wait_recv()

    def cross_products(h, sx):
        hs = lanes(h)
        sx[0] = mm(x[1, :, hs], pr[0, :, hs], NT) * SCALE2
        sx[1] = mm(x[2, :, hs], pr[3, :, hs], NT)

    def cross_weigh(h, sx, pd):
        lse = lr[0, pl.ds(h, 1), :]
        delta = lr[1, pl.ds(h, 1), :]
        s2 = sx[0].reshape(TOK // 8, 8, HALF)
        x2 = sx[1].reshape(TOK // 8, 8, HALF)
        p2 = jnp.exp2(jnp.where(parity_sub[:, :, :HALF] == off[0, h], s2 - lse, LOW))
        pd[0] = p2.reshape(TOK, HALF).astype(BF16)
        pd[1] = ((p2 * FACTOR) * (x2 - delta)).reshape(TOK, HALF).astype(BF16)

    def cross_gather(h, pd):
        hs = lanes(h)
        acc[2, :, hs] += mm(pd[0], pr[3, :, hs], NN)
        acc[1, :, hs] += mm(pd[1], pr[0, :, hs], NN)

    def cross_two(j):
        cross_gather(2 * j - 1, eb)
        cross_weigh(2 * j, ua, ea)
        cross_products(2 * j + 1, ub)
        cross_gather(2 * j, ea)
        cross_weigh(2 * j + 1, ub, eb)
        cross_products(jnp.minimum(2 * j + 2, HEADS - 1), ua)

    cross_products(0, ua)
    cross_weigh(0, ua, ea)
    cross_products(1, ub)
    cross_gather(0, ea)
    cross_weigh(1, ub, eb)
    cross_products(2, ua)

    @pl.loop(1, CROSS_FIRST)
    def _(j):
        cross_two(j)

    def to_member(d):
        shift = (zs[d // 2 % 2] + cs[d % 2])
        j = lax.rem(y + d // 4, 4) * 4 + shift
        return remote(
            rs.at[rows_of(j)], rb.at[rows_of(mine)], p3_send.at[d], p3_recv, (plane + ys[d // 4] + shift,)
        )

    @pl.when(owner)
    def _():
        seven = pl.ds(0, ZGROUPS - 1)
        pltpu.make_async_copy(tt.at[seven], tt.at[seven], p2_recv).wait()
        qw, kw, vw, gw = [tt[:, i].reshape(128, DH) for i in range(4)]
        s = mm(kw, qw, NT) * SCALE2
        xx = mm(vw, gw, NT)
        top = jnp.max(s, 0, keepdims=True)
        e = jnp.exp2(s - top)
        tot = jnp.sum(e, 0, keepdims=True)
        num = jnp.sum(e * xx, 0, keepdims=True)
        pltpu.make_async_copy(ts.at[seven], ts.at[seven], c2_recv).wait()
        stat = jnp.sum(ts[...], 0)
        near, near_delta, far, far_delta = [stat[i : i + 1] for i in range(4)]
        peak = jnp.maximum(top, jnp.maximum(near, far))
        c_w = jnp.exp2(top - peak)
        c_near = jnp.exp2(near - peak)
        c_far = jnp.exp2(far - peak)
        all_tot = tot * c_w + (c_near + c_far)
        lse = peak + jnp.log2(all_tot)
        delta = (num * c_w + (near_delta * c_near + far_delta * c_far)) / all_tot
        p = e * (c_w / all_tot)
        ds = ((p * FACTOR) * (xx - delta)).astype(BF16)
        wd[0] = mm(ds, kw, TN)
        wd[1] = mm(ds, qw, NN)
        wd[2] = mm(p.astype(BF16), gw, NN)
        own = pl.ds(pl.multiple_of(zg * GROUP, GROUP), GROUP)
        for i in range(3):
            rs[pl.ds(i, GROUP, stride=8), :] = wd[i, own, :]
        rs[pl.ds(3, GROUP, stride=8), :] = jnp.broadcast_to(lse, (GROUP, DH))
        rs[pl.ds(4, GROUP, stride=8), :] = jnp.broadcast_to(delta, (GROUP, DH))

        for d in (10, 11, 9, 8, 6, 7, 14, 15, 4, 5, 12, 13, 2, 3, 1):
            to_member(d).start()

        pltpu.make_async_copy(rs.at[rows_of(m)], rb.at[rows_of(mine)], p3_recv).start()

    @pl.loop(CROSS_FIRST, PAIRS)
    def _(j):
        cross_two(j)

    cross_gather(HEADS - 1, eb)

    wx[0] = jnp.where(row_in_pair[:, :HALF], mm(qr[0], pr[1], NT) * SCALE2, LOW)
    wx[1] = mm(qr[3], pr[2], NT)

    for copy in pair_copies + wide_copies:
        copy.wait_send()
    stat_copy.wait_send()
    wait_sent(sb, pb, p1_send, p1_recv)
    wait_sent(sc, pc, c1_send, c1_recv)

    @pl.when(owner)
    def _():
        for d in range(1, ZGROUPS):
            to_zpeer(tt, p2_send, p2_recv, d).wait_send()
            to_zpeer(ts, c2_send, c2_recv, d).wait_send()

        for d in range(1, GROUP):
            to_member(d).wait_send()

    got = pl.ds(0, 8 * HEADS)
    pltpu.make_async_copy(rb.at[got], rb.at[got], p3_recv).wait()

    all_lse = rb[pl.ds(3, 16, stride=8), :]
    all_delta = rb[pl.ds(4, 16, stride=8), :]
    def at(mask, value):
        return jnp.sum(jnp.where(mask, value, 0.0), 1, keepdims=True)

    lse_r, delta_r = at(here, all_lse), at(here, all_delta)
    lse_f, delta_f = at(other, all_lse), at(other, all_delta)
    p_own = jnp.exp2(ws[0] - lse_r) * weight_wide
    d_own = ((p_own * FACTOR) * (ws[1] - delta_r)).astype(BF16)
    p_cross = jnp.exp2(wx[0] - lse_r)
    d_cross = ((p_cross * FACTOR) * (wx[1] - delta_r)).astype(BF16)
    p_far = jnp.exp2(w2[0] - lse_f)
    d_far = ((p_far * FACTOR) * (w2[1] - delta_f)).astype(BF16)

    def spread(i):
        row = rb[pl.ds(i, 16, stride=8), :]
        return jnp.where(block, jnp.concatenate([row] * HEADS, axis=1), 0.0)

    dq_row = jnp.where(block, mm(d_own, x[1], NN) + mm(d_cross, pr[1], NN), 0.0) + spread(0)
    sel = sel_wide
    blank_left = jnp.zeros((32, TOK), BF16)
    blank_right = jnp.zeros((32, WIDTH), BF16)
    left[0] = jnp.concatenate([sel, sel, blank_left], 0)
    fix[0] = jnp.concatenate([*split(dq_row), blank_right], 0)
    left[1] = jnp.concatenate([d_own, d_far, sel, sel], 0)
    fix[1] = jnp.concatenate([qr[0], qp[0], *split(spread(1))], 0)
    left[2] = jnp.concatenate([p_own.astype(BF16), p_far.astype(BF16), sel, sel], 0)
    fix[2] = jnp.concatenate([qr[3], qp[1], *split(spread(2))], 0)


def finish(acc, left, fix, oq, ok, ov, held, sem):
    stores = []
    for i, ref in enumerate((oq, ok, ov)):
        for part in range(2):
            rows = pl.ds(part * HALF, HALF)
            held[i, rows, :] = (acc[i, rows, :] + mm(left[i, :, rows], fix[i], TN)).astype(BF16)
            stores.append(pltpu.make_async_copy(held.at[i, rows], ref.at[rows], sem.at[2 * i + part]))
            stores[-1].start()
    for store in stores:
        store.wait()


def on_device(query, key, value, grad_out, offsets):
    shape = jax.ShapeDtypeStruct((TOK, WIDTH), BF16)
    vmem = pltpu.VMEM
    dma = pltpu.SemaphoreType.DMA
    acc, left, fix = pl.pallas_call(
        kernel,
        out_shape=(
            jax.ShapeDtypeStruct((3, TOK, WIDTH), F32),
            jax.ShapeDtypeStruct((3, 64, TOK), BF16),
            jax.ShapeDtypeStruct((3, 64, WIDTH), BF16),
        ),
        in_specs=[pl.BlockSpec(memory_space=pltpu.MemorySpace.HBM)] * 5,
        out_specs=(pl.BlockSpec(memory_space=vmem),) * 3,
        scratch_shapes=[
            vmem((4, TOK, WIDTH), BF16),
            vmem((4, HALF, WIDTH), BF16),
            vmem((4, HALF, WIDTH), BF16),
            vmem((4, 16, WIDTH), BF16),
            vmem((8 * HEADS, DH), F32),
            vmem((8 * GROUP, DH), F32),
            vmem((8 * HEADS, DH), F32),
            vmem((8 * GROUP, DH), F32),
            vmem((ZGROUPS, 4, GROUP, DH), BF16),
            vmem((ZGROUPS, 4, DH), F32),
            vmem((8 * GROUP, DH), F32),
            vmem((8 * 16, DH), F32),
            vmem((2, 16, HALF), F32),
            vmem((2, 16, HALF), F32),
            vmem((2, 16, TOK), F32),
            vmem((2, 16, TOK), F32),
            vmem((2, 16, HALF), F32),
            vmem((2, 16, TOK), F32),
            vmem((2, 16, WIDTH), BF16),
            vmem((3, 128, DH), F32),
            pltpu.SMEM((2, HEADS), jnp.int32),
            vmem((2, TOK + HALF, TOK), F32),
            vmem((2, TOK + HALF, TOK), F32),
            vmem((1, TOK), F32),
            vmem((1, TOK), F32),
            vmem((2 * TOK + HALF, TOK), BF16),
            vmem((2 * TOK + HALF, TOK), BF16),
            vmem((2, TOK, HALF), F32),
            vmem((2, TOK, HALF), F32),
            vmem((2, TOK, HALF), BF16),
            vmem((2, TOK, HALF), BF16),
            dma((4,)),
            dma(()),
            pltpu.SemaphoreType.REGULAR((2,)),
            dma((4,)),
            dma((4,)),
            dma((HEADS,)),
            dma(()),
            dma((HEADS,)),
            dma(()),
            dma((ZGROUPS,)),
            dma(()),
            dma((ZGROUPS,)),
            dma(()),
            dma((GROUP,)),
            dma(()),
            dma(()),
            dma(()),
            dma((2,)),
            dma((2,)),
        ],
        compiler_params=pltpu.CompilerParams(collective_id=0, has_side_effects=True, vmem_limit_bytes=48 * 1024 * 1024),
    )(*[pltpu.with_memory_space_constraint(a, pltpu.MemorySpace.HBM) for a in (offsets, query, key, value, grad_out)])
    return pl.pallas_call(
        finish,
        out_shape=(shape, shape, shape),
        in_specs=[pl.BlockSpec(memory_space=vmem)] * 3,
        out_specs=(pl.BlockSpec(memory_space=pl.ANY),) * 3,
        scratch_shapes=[vmem((3, TOK, WIDTH), BF16), dma((6,))],
        compiler_params=pltpu.CompilerParams(vmem_limit_bytes=8 * 1024 * 1024),
    )(acc, left, fix)


def solution(mesh):
    placed = (P("ctx", None),) * 4 + (P(),)
    return jax.shard_map(
        on_device, mesh=mesh, in_specs=placed, out_specs=(P("ctx", None),) * 3, check_vma=False
    )
```

time: 35.8 us -> 34.4 us (0.961)
  Pallas kernels: 35 us -> 33.6 us
    pallas_call x1, Pallas kernels: 33.4 us -> 32 us  [on_device(): pl.pallas_call(kernel, out_shape=(jax.ShapeDtypeStruct((3, TOK, WIDTH), F...]
where the time goes in v4:
time: 34.4 us; the launch traced here: 34.3 us
  Pallas kernels  33.6 us (98%)
  between operations  0.64 us (2%)
    pallas_call x1, Pallas kernels, on_device(): pl.pallas_call(kernel, out_shape=(jax.ShapeDtypeStruct((3, TOK, WIDTH), F...  32 us
    pallas_call x1, Pallas kernels, on_device(): pl.pallas_call(finish, out_shape=(shape, shape, shape), in_specs=[pl.Bloc...  1.6 us

profile of v4, /device:TPU:1, one launch (start us, length us, event | category | flops | bytes accessed | tf_op | source)
XLA Modules:
  0.0 34.3 jit_solution(12516842312051265656)
XLA Ops:
  0.6 32.0 %shard_map.76 = (f32[3,256,1280]{2,1,0:T(8,128)S(1)}, bf16[3,64,256]{2,1,0:T(8,128)(2,1)S(1)}, bf16[3,64,1280]{2,1,0:T(8,128)(2,1)S(1)}) custom-call(s32[2,10]{1,0:T(2,128)} %off_hbm.1, bf16[256,1280]{1,0:T(8,128)(2,1)} %q_hbm.1, bf16[256,1280]{1,0:T(8,128)(2,1)} %k_hbm.1, bf16[256,1280]{1,0:T(8,128)(2,1)} %v_hbm.1, bf16[256,1280]{1,0:T(8,128)(2,1)} %g_hbm.1), custom_call_target="tpu_custom_call" | custom-call | tf_op jit(solution)/shard_map/pallas_call | solution.py:497
  32.7 1.6 %shard_map.77 = (bf16[256,1280]{1,0:T(8,128)(2,1)}, bf16[256,1280]{1,0:T(8,128)(2,1)}, bf16[256,1280]{1,0:T(8,128)(2,1)}) custom-call(f32[3,256,1280]{2,1,0:T(8,128)S(1)} %get-tuple-element.6.acc, bf16[3,64,256]{2,1,0:T(8,128)(2,1)S(1)} %get-tuple-element.7.left, bf16[3,64,1280]{2,1,0:T(8,128)(2,1)S(1)} %get-tuple-element.8.fix), custom_call_target="tpu_custom_call" | custom-call | tf_op jit(solution)/shard_map/pallas_call | solution.py:560

commit v5 on v4

--- a/solution.py
+++ b/solution.py
@@ -108,12 +108,6 @@
             pl.semaphore_signal(ready.at[0], inc=1, device_id=upper2, device_id_type=MESH)
             pl.semaphore_signal(ready.at[1], inc=1, device_id=lower2, device_id_type=MESH)
 
-    def far_groups_ready():
-        @pl.when(owner)
-        def _():
-            pl.semaphore_wait(ready.at[0], 1)
-            pl.semaphore_wait(ready.at[1], 1)
-
     sb[...] = jnp.zeros_like(sb)
     sc[...] = jnp.zeros_like(sc)
     rb[...] = jnp.zeros_like(rb)
@@ -161,9 +155,9 @@
             def _():
                 to_owner(src, dst, send, recv, h).start()
 
-            @pl.when(owner_of(h) == m)
-            def _():
-                pltpu.make_async_copy(src.at[rows_of(h)], dst.at[rows_of(m)], recv).start()
+        @pl.when(owner)
+        def _():
+            pltpu.make_async_copy(src.at[rows_of(mine)], dst.at[rows_of(m)], recv).start()
 
     def wait_sent(src, dst, send, recv):
         @pl.loop(0, HEADS)
@@ -218,12 +212,9 @@
 
     for copy in wide_copies:
         copy.wait_recv()
-    s_far = jnp.where(both, mm(qp[0], x[1], NT) * SCALE2, LOW)
-    x_far = mm(qp[1], x[2], NT)
-    statistics(s_far, x_far, None, 2, other)
+    s_far = jnp.where(row_in_pair[:, :HALF], mm(qp[0], px[1], NT) * SCALE2, LOW)
+    statistics(s_far, mm(qp[1], px[2], NT), None, 2, other)
     send_to_owners(sc, pc, c1_send, c1_recv)
-    w2[0] = s_far
-    w2[1] = x_far
 
     pack_pair(0)
     pair_copies[0].start()
@@ -287,13 +278,16 @@
     def to_zpeer(src, send, recv, d):
         return remote(src.at[zg], src.at[zg], send.at[d], recv, zpeer(d))
 
-    far_groups_ready()
     @pl.when(owner)
     def _():
         pltpu.make_async_copy(pb, pb, p1_recv).wait()
         for i in range(4):
             tt[zg, i] = pb[pl.ds(i, GROUP, stride=8), :].astype(BF16)
-        for d in (4, 3, 5, 2, 6, 1, 7):
+        for d in (2, 6):
+            to_zpeer(tt, p2_send, p2_recv, d).start()
+        pl.semaphore_wait(ready.at[0], 1)
+        pl.semaphore_wait(ready.at[1], 1)
+        for d in (4, 3, 5):
             to_zpeer(tt, p2_send, p2_recv, d).start()
 
     pair_copies[1].wait_recv()
@@ -312,6 +306,8 @@
             ts[zg, i : i + 1, :] = jnp.sum(pc[pl.ds(i, GROUP, stride=8), :], 0, keepdims=True)
         for d in (4, 3, 5, 2, 6, 1, 7):
             to_zpeer(ts, c2_send, c2_recv, d).start()
+        for d in (1, 7):
+            to_zpeer(tt, p2_send, p2_recv, d).start()
 
     @pl.loop(1, PAIRS)
     def _(j):
@@ -376,6 +372,11 @@
     @pl.loop(1, CROSS_FIRST)
     def _(j):
         cross_two(j)
+
+    wx[0] = jnp.where(row_in_pair[:, :HALF], mm(qr[0], pr[1], NT) * SCALE2, LOW)
+    wx[1] = mm(qr[3], pr[2], NT)
+    w2[0] = jnp.where(both, mm(qp[0], x[1], NT) * SCALE2, LOW)
+    w2[1] = mm(qp[1], x[2], NT)
 
     def to_member(d):
         shift = (zs[d // 2 % 2] + cs[d % 2])
@@ -426,9 +427,6 @@
         cross_two(j)
 
     cross_gather(HEADS - 1, eb)
-
-    wx[0] = jnp.where(row_in_pair[:, :HALF], mm(qr[0], pr[1], NT) * SCALE2, LOW)
-    wx[1] = mm(qr[3], pr[2], NT)
 
     for copy in pair_copies + wide_copies:
         copy.wait_send()

time: 34.4 us -> 34.5 us (level)
  no operation moved by 1% of the time
where the time goes in v5:
time: 34.5 us; the launch traced here: 34.4 us
  Pallas kernels  33.7 us (98%)
  between operations  0.64 us (2%)
    pallas_call x1, Pallas kernels, on_device(): pl.pallas_call(kernel, out_shape=(jax.ShapeDtypeStruct((3, TOK, WIDTH), F...  32.1 us
    pallas_call x1, Pallas kernels, on_device(): pl.pallas_call(finish, out_shape=(shape, shape, shape), in_specs=[pl.Bloc...  1.61 us

profile of v5, /device:TPU:1, one launch (start us, length us, event | category | flops | bytes accessed | tf_op | source)
XLA Modules:
  0.0 34.4 jit_solution(11051773722342578083)
XLA Ops:
  0.6 32.1 %shard_map.76 = (f32[3,256,1280]{2,1,0:T(8,128)S(1)}, bf16[3,64,256]{2,1,0:T(8,128)(2,1)S(1)}, bf16[3,64,1280]{2,1,0:T(8,128)(2,1)S(1)}) custom-call(s32[2,10]{1,0:T(2,128)} %off_hbm.1, bf16[256,1280]{1,0:T(8,128)(2,1)} %q_hbm.1, bf16[256,1280]{1,0:T(8,128)(2,1)} %k_hbm.1, bf16[256,1280]{1,0:T(8,128)(2,1)} %v_hbm.1, bf16[256,1280]{1,0:T(8,128)(2,1)} %g_hbm.1), custom_call_target="tpu_custom_call" | custom-call | tf_op jit(solution)/shard_map/pallas_call | solution.py:495
  32.8 1.6 %shard_map.77 = (bf16[256,1280]{1,0:T(8,128)(2,1)}, bf16[256,1280]{1,0:T(8,128)(2,1)}, bf16[256,1280]{1,0:T(8,128)(2,1)}) custom-call(f32[3,256,1280]{2,1,0:T(8,128)S(1)} %get-tuple-element.6.acc, bf16[3,64,256]{2,1,0:T(8,128)(2,1)S(1)} %get-tuple-element.7.left, bf16[3,64,1280]{2,1,0:T(8,128)(2,1)S(1)} %get-tuple-element.8.fix), custom_call_target="tpu_custom_call" | custom-call | tf_op jit(solution)/shard_map/pallas_call | solution.py:558
